TPU v7x, 32 devices: a whole 2x2x4 slice. The times are simulated.
32 devices in a mesh: dp: 2 (over x), var: 4 (over y, core), mp: 4 (over z).
Axes of the slice: x: 2, y: 2, z: 4, core: 2. Of those that a mesh axis runs over, the one named last changes fastest.
Arguments:
- fields: bfloat16 [4, 48, 4, 512], P('dp', 'var'), may hold values from -6 to 6
- target: float32 [4, 512, 192], P('dp'), may hold values from -6 to 6
- lead_hours: int32 [4], P('dp'), may hold values from 6 to 168
- sources: int32 [4], replicated, may hold values from 0 to 4
- variables: int32 [48], P('var'), may hold values from 0 to 47, each once
- step_count: int32 [], replicated, may hold values from 2 to 20
- attention_weight: float32 [4, 1024, 1024], P(None, 'dp', ('var', 'mp')), may hold values from -0.1875 to 0.1875
- attention_moment: float32 [4, 1024, 1024], P(None, 'dp', ('var', 'mp')), may hold values from -1.9073486e-05 to 1.9073486e-05
- attention_square: float32 [4, 1024, 1024], P(None, 'dp', ('var', 'mp')), may hold values from 4.190733e-12 to 1.6665471e-11
- dense_weight: float32 [2, 1024, 4096], P(None, 'dp', ('var', 'mp')), may hold values from -0.1875 to 0.1875
- dense_moment: float32 [2, 1024, 4096], P(None, 'dp', ('var', 'mp')), may hold values from -1.9073486e-05 to 1.9073486e-05
- dense_square: float32 [2, 1024, 4096], P(None, 'dp', ('var', 'mp')), may hold values from 4.190733e-12 to 1.6665471e-11
- mixing_weight: float32 [3, 1024, 1024], P(None, ('dp', 'var'), 'mp'), may hold values from -0.1875 to 0.1875
- mixing_moment: float32 [3, 1024, 1024], P(None, ('dp', 'var'), 'mp'), may hold values from -1.9073486e-05 to 1.9073486e-05
- mixing_square: float32 [3, 1024, 1024], P(None, ('dp', 'var'), 'mp'), may hold values from 4.190733e-12 to 1.6665471e-11
- norm_gains: float32 [5, 1024], P(None, ('dp', 'var', 'mp')), may hold values from 0.5 to 1.5
- gains_moment: float32 [5, 1024], P(None, ('dp', 'var', 'mp')), may hold values from -7.6293945e-05 to 7.6293945e-05
- gains_square: float32 [5, 1024], P(None, ('dp', 'var', 'mp')), may hold values from 6.7051725e-11 to 2.6664754e-10
- position_table: float32 [512, 1024], P(None, ('dp', 'var', 'mp')), may hold values from -3 to 3
- position_moment: float32 [512, 1024], P(None, ('dp', 'var', 'mp')), may hold values from -5.9604645e-07 to 5.9604645e-07
- position_square: float32 [512, 1024], P(None, ('dp', 'var', 'mp')), may hold values from 4.2913103e-15 to 1.7065444e-14
- head_weight: float32 [192, 1024], P(None, ('dp', 'var', 'mp')), may hold values from -0.1875 to 0.1875
- head_moment: float32 [192, 1024], P(None, ('dp', 'var', 'mp')), may hold values from -7.6293945e-05 to 7.6293945e-05
- head_square: float32 [192, 1024], P(None, ('dp', 'var', 'mp')), may hold values from 6.7051725e-11 to 2.6664754e-10
- embed_table: float32 [240, 1024], P(None, ('dp', 'var', 'mp')), may hold values from -3 to 3
- embed_moment: float32 [240, 1024], P(None, ('dp', 'var', 'mp')), may hold values from -3.8146973e-06 to 3.8146973e-06
- embed_square: float32 [240, 1024], P(None, ('dp', 'var', 'mp')), may hold values from 1.6762931e-13 to 6.666189e-13
Outputs:
- loss_value: float32 [], replicated
- grad_norm: float32 [], replicated
- attention_new: float32 [4, 1024, 1024], P(None, 'dp', ('var', 'mp'))
- attention_moment_new: float32 [4, 1024, 1024], P(None, 'dp', ('var', 'mp'))
- attention_square_new: float32 [4, 1024, 1024], P(None, 'dp', ('var', 'mp'))
- dense_new: float32 [2, 1024, 4096], P(None, 'dp', ('var', 'mp'))
- dense_moment_new: float32 [2, 1024, 4096], P(None, 'dp', ('var', 'mp'))
- dense_square_new: float32 [2, 1024, 4096], P(None, 'dp', ('var', 'mp'))
- mixing_new: float32 [3, 1024, 1024], P(None, ('dp', 'var'), 'mp')
- mixing_moment_new: float32 [3, 1024, 1024], P(None, ('dp', 'var'), 'mp')
- mixing_square_new: float32 [3, 1024, 1024], P(None, ('dp', 'var'), 'mp')
- gains_new: float32 [5, 1024], P(None, ('dp', 'var', 'mp'))
- gains_moment_new: float32 [5, 1024], P(None, ('dp', 'var', 'mp'))
- gains_square_new: float32 [5, 1024], P(None, ('dp', 'var', 'mp'))
- position_new: float32 [512, 1024], P(None, ('dp', 'var', 'mp'))
- position_moment_new: float32 [512, 1024], P(None, ('dp', 'var', 'mp'))
- position_square_new: float32 [512, 1024], P(None, ('dp', 'var', 'mp'))
- head_new: float32 [192, 1024], P(None, ('dp', 'var', 'mp'))
- head_moment_new: float32 [192, 1024], P(None, ('dp', 'var', 'mp'))
- head_square_new: float32 [192, 1024], P(None, ('dp', 'var', 'mp'))
- embed_new: float32 [240, 1024], P(None, ('dp', 'var', 'mp'))
- embed_moment_new: float32 [240, 1024], P(None, ('dp', 'var', 'mp'))
- embed_square_new: float32 [240, 1024], P(None, ('dp', 'var', 'mp'))
- stream_rms: float32 [4], replicated
Inputs may be any that keep to these rules, and one draw needn't show every extreme that they name: variables is a permutation of the 48 variables.
All inputs are finite; a program needn't handle non-finite values.
Results may differ from a plain program's by a relative error of at most 0.023.
Values may be sent and summed in bfloat16 or wider, within the bound.
A program may use at most 256 MiB of HBM per device.

v0:
```python
import math

import jax
import jax.numpy as jnp
from jax import lax
from jax.sharding import PartitionSpec as P

D = 1024
HEADS = 16
VARS = 48
PIX = 4
PH = 16
PW = 32
NSRC = 5
P_SIZE = 512


HIGHEST = lax.Precision.HIGHEST
FLOAT = jnp.float32
BFLOAT = jnp.bfloat16
NORM_EPS = 1e-05
BETA_ONE = 0.5
BETA_TWO = 0.7
ADAM_EPS = 1e-08
DECAY = 0.01


def combined_all(value, axis, combine):
    everything = jax.tree.map(
        lambda part, kind: lax.all_gather(part.astype(kind), axis),
        value,
        (jnp.bfloat16, jnp.bfloat16, jnp.bfloat16),
    )

    def take(k):
        return jax.tree.map(lambda part, own: part[k].astype(own.dtype), everything, value)

    return lax.fori_loop(
        1, lax.axis_size(axis), lambda k, so_far: combine(so_far, take(k)), take(0)
    )


def widen(per_head):
    return jnp.repeat(per_head, D // HEADS, axis=-1)


def combine_softmax(first_part, second_part):
    first_max, first_total, first_mix = first_part
    second_max, second_total, second_mix = second_part
    joint_max = jnp.maximum(first_max, second_max)
    first_scale = jnp.exp(first_max - joint_max)
    second_scale = jnp.exp(second_max - joint_max)
    return (
        joint_max,
        first_total * first_scale + second_total * second_scale,
        first_mix * widen(first_scale) + second_mix * widen(second_scale),
    )


def norm_forward(values, gain_row):
    centred = values - jnp.mean(values, -1, keepdims=True)
    inverse = lax.rsqrt(jnp.mean(centred * centred, -1, keepdims=True) + NORM_EPS)
    unit_rows = centred * inverse
    return (unit_rows * gain_row, unit_rows, inverse)


def norm_backward(grad_out, unit_rows, inverse, gain_row):
    scaled = grad_out * gain_row
    return inverse * (
        scaled
        - jnp.mean(scaled, -1, keepdims=True)
        - unit_rows * jnp.mean(scaled * unit_rows, -1, keepdims=True)
    )


def gelu_exact(values):
    return jax.nn.gelu(values, approximate=False)


def gelu_back(values, grad_out):
    _, pullback = jax.vjp(gelu_exact, values)
    return pullback(grad_out)[0]


def latitude_weights():
    angles = (jnp.arange(PH, dtype=FLOAT) + 0.5) * (math.pi / PH) - math.pi / 2
    cosine = jnp.cos(angles)
    return jnp.repeat(cosine / jnp.mean(cosine), PW)


def self_scores(queries, keys_in):
    return jnp.einsum(
        "iqhk,ithk->ihqt", queries, keys_in, preferred_element_type=FLOAT
    ) / math.sqrt(D // HEADS)


def adam_update(weight, gradient, first_moment, second, factor, step_value, step_rate, decay_rate):
    clipped = gradient * factor
    first_moment = BETA_ONE * first_moment + (1.0 - BETA_ONE) * clipped
    second = BETA_TWO * second + (1.0 - BETA_TWO) * clipped * clipped
    normalized = (
        first_moment
        / (1.0 - jnp.power(BETA_ONE, step_value))
        / (jnp.sqrt(second / (1.0 - jnp.power(BETA_TWO, step_value))) + ADAM_EPS)
    )
    return (weight - step_rate * (normalized + decay_rate * weight), first_moment, second)


def body(
    fields,
    target,
    lead_hours,
    sources,
    variables,
    step_count,
    attention_weight,
    attention_moment,
    attention_square,
    dense_weight,
    dense_moment,
    dense_square,
    mixing_weight,
    mixing_moment,
    mixing_square,
    norm_gains,
    gains_moment,
    gains_square,
    position_table,
    position_moment,
    position_square,
    head_weight,
    head_moment,
    head_square,
    embed_table,
    embed_moment,
    embed_square,
):
    head_dim = D // HEADS
    root_dim = math.sqrt(head_dim)
    groups = lax.axis_size("var") * lax.axis_size("mp")
    local_items = fields.shape[0]
    local_vars = fields.shape[1]
    total_rows = local_items * P_SIZE
    share_rows = total_rows // groups
    variable_rows = total_rows // lax.axis_size("var")
    share_start = lax.axis_index(("var", "mp")) * share_rows
    mixing_cols = D // lax.axis_size("mp")
    mixing_heads = mixing_cols // head_dim
    items_all = sources.shape[0]

    def rows_share(full_rows):
        return lax.dynamic_slice_in_dim(full_rows, share_start, share_rows, 0)

    def mine(held_rows):
        return rows_share(held_rows)

    def sum_forward(partial_rows):
        return lax.psum(partial_rows.astype(jnp.bfloat16), ("var", "mp")).astype(jnp.float32)

    def sum_backward(partial_rows):
        return lax.psum(partial_rows.astype(jnp.bfloat16), ("var", "mp")).astype(jnp.float32)

    attention_all, dense_all = (
        lax.all_gather(attention_weight.astype(BFLOAT), "dp", axis=1, tiled=True),
        lax.all_gather(dense_weight.astype(BFLOAT), "dp", axis=1, tiled=True),
    )
    mixing_all = lax.all_gather(mixing_weight.astype(BFLOAT), ("dp", "var"), axis=1, tiled=True)
    gains_all, position_all, head_all, embed_all = (
        lax.all_gather(norm_gains, ("dp", "var", "mp"), axis=1, tiled=True),
        lax.all_gather(position_table, ("dp", "var", "mp"), axis=1, tiled=True),
        lax.all_gather(head_weight, ("dp", "var", "mp"), axis=1, tiled=True),
        lax.all_gather(embed_table, ("dp", "var", "mp"), axis=1, tiled=True),
    )
    slot_pick = (variables[:, None] == jnp.arange(VARS)[None, :]).astype(FLOAT)
    slot_table = jnp.einsum(
        "jv,vcd->jcd", slot_pick, embed_all.reshape(VARS, PIX + 1, D), precision=HIGHEST
    )
    field_ones = jnp.concatenate(
        [fields, jnp.ones((local_items, local_vars, 1, P_SIZE), BFLOAT)], 2
    )
    embeds = (
        jnp.einsum("ijcp,jcd->jipd", field_ones.astype(FLOAT), slot_table, precision=HIGHEST)
        .reshape(local_vars, total_rows, D)
        .astype(BFLOAT)
    )
    key_matrix = mixing_all[0]
    value_matrix = mixing_all[1]
    out_matrix = mixing_all[2]
    mp_start = lax.axis_index("mp") * mixing_cols
    query_local = lax.dynamic_slice_in_dim(gains_all[4], mp_start, mixing_cols, 0).reshape(
        mixing_heads, head_dim
    )
    key_query = jnp.einsum(
        "dhk,hk->dh",
        key_matrix.astype(FLOAT).reshape(D, mixing_heads, head_dim),
        query_local,
        precision=HIGHEST,
    ).astype(BFLOAT)
    variable_scores = (
        jnp.einsum("jrd,dh->jrh", embeds, key_query, preferred_element_type=FLOAT) / root_dim
    )
    variable_values = jnp.einsum(
        "jrd,de->jre", embeds, value_matrix, preferred_element_type=FLOAT
    ).astype(BFLOAT)
    local_max = jnp.max(variable_scores, 0)
    local_exp = jnp.exp(variable_scores - local_max[None])
    local_total = jnp.sum(local_exp, 0)
    local_mix = jnp.sum(widen(local_exp) * variable_values, 0)
    merged_max, merged_total, merged_mix = combined_all(
        (local_max, local_total, local_mix), "var", combine_softmax
    )
    mixed_float = merged_mix / widen(merged_total)
    mixed_rows = mixed_float.astype(BFLOAT)
    log_total = merged_max + jnp.log(merged_total)
    var_start = lax.axis_index("var") * variable_rows
    start_part = jnp.einsum("re,de->rd", mixed_rows, out_matrix, preferred_element_type=FLOAT)
    start_rows = lax.psum(start_part.astype(jnp.bfloat16), "mp").astype(jnp.float32)
    item_first = lax.axis_index("dp") * local_items
    own_sources = lax.dynamic_slice_in_dim(sources, item_first, local_items, 0)
    counts = jnp.sum((sources[:, None] == jnp.arange(NSRC)[None, :]).astype(FLOAT), 0)
    item_count = jnp.sum(
        (own_sources[:, None] == jnp.arange(NSRC)[None, :]).astype(FLOAT) * counts[None, :], 1
    )
    row_scale = jnp.repeat(1.0 / (NSRC * P_SIZE * PIX * VARS * item_count), P_SIZE)
    lead_rows = jnp.repeat(lead_hours.astype(FLOAT) / 100.0, P_SIZE)
    row_latitude = jnp.tile(latitude_weights(), local_items)
    row_patch = jnp.tile(jnp.arange(P_SIZE), local_items)
    residual0 = (
        start_rows + jnp.tile(position_all, (local_items, 1)) + lead_rows[:, None] * gains_all[3]
    )
    normed1, unit1, inverse1 = norm_forward(residual0, gains_all[0])
    normed1_all = normed1.astype(BFLOAT)
    head_cols = attention_all.shape[2]
    local_heads = head_cols // head_dim
    qkv_matrix = attention_all[:3].transpose(1, 0, 2).reshape(D, 3 * head_cols)
    projected = jnp.dot(normed1_all, qkv_matrix, preferred_element_type=FLOAT).astype(BFLOAT)
    heads_view = projected.reshape(local_items, P_SIZE, 3, local_heads, head_dim)
    queries = heads_view[:, :, 0]
    keys_in = heads_view[:, :, 1]
    values_in = heads_view[:, :, 2]
    raw_scores = self_scores(queries, keys_in)
    row_max = jnp.max(raw_scores, -1, keepdims=True)
    shifted = jnp.exp(raw_scores - row_max)
    row_total = jnp.sum(shifted, -1, keepdims=True)
    log_norm = row_max + jnp.log(row_total)
    soft_weights = (shifted / row_total).astype(BFLOAT)
    attended = (
        jnp.einsum("ihqt,ithk->iqhk", soft_weights, values_in, preferred_element_type=FLOAT)
        .reshape(total_rows, head_cols)
        .astype(BFLOAT)
    )
    attend_out = sum_forward(
        jnp.einsum("re,de->rd", attended, attention_all[3], preferred_element_type=FLOAT)
    )
    residual1 = residual0 + attend_out
    normed2, unit2, inverse2 = norm_forward(residual1, gains_all[1])
    normed2_all = normed2.astype(BFLOAT)
    pre_act = jnp.dot(normed2_all, dense_all[0], preferred_element_type=FLOAT)
    activated = gelu_exact(pre_act).astype(BFLOAT)
    dense_out = sum_forward(
        jnp.einsum("rf,df->rd", activated, dense_all[1], preferred_element_type=FLOAT)
    )
    residual2 = residual1 + dense_out
    normed3, unit3, inverse3 = norm_forward(residual2, gains_all[2])
    normed3_low = normed3.astype(BFLOAT)
    head_low = head_all.astype(BFLOAT)
    predicted = jnp.einsum("rd,cd->rc", normed3_low, head_low, preferred_element_type=FLOAT)
    errors = predicted - target.reshape(total_rows, PIX * VARS)
    weight_rows = row_scale * row_latitude
    loss_part = jnp.sum(mine(weight_rows[:, None] * errors * errors))
    grad_pred = 2.0 * weight_rows[:, None] * errors
    grad_normed3 = jnp.dot(grad_pred, head_low.astype(FLOAT), precision=HIGHEST)
    grad_head = jnp.einsum(
        "rc,rd->cd", mine(grad_pred), mine(normed3_low).astype(FLOAT), precision=HIGHEST
    )
    grad_gain3 = jnp.sum(mine(grad_normed3 * unit3), 0)
    grad_residual2 = norm_backward(grad_normed3, unit3, inverse3, gains_all[2])
    dense_grad_all = grad_residual2.astype(BFLOAT)
    grad_activated = jnp.dot(dense_grad_all, dense_all[1], preferred_element_type=FLOAT)
    grad_down = jnp.einsum("rd,rf->df", dense_grad_all, activated, preferred_element_type=FLOAT)
    grad_pre = gelu_back(pre_act, grad_activated).astype(BFLOAT)
    grad_up = jnp.einsum("rd,rf->df", normed2_all, grad_pre, preferred_element_type=FLOAT)
    grad_normed2 = sum_backward(
        jnp.einsum("rf,df->rd", grad_pre, dense_all[0], preferred_element_type=FLOAT)
    )
    grad_gain2 = jnp.sum(mine(grad_normed2 * unit2), 0)
    grad_residual1 = grad_residual2 + norm_backward(grad_normed2, unit2, inverse2, gains_all[1])
    attend_grad_all = grad_residual1.astype(BFLOAT)
    grad_out_proj = jnp.einsum("rd,re->de", attend_grad_all, attended, preferred_element_type=FLOAT)
    grad_attended = jnp.dot(attend_grad_all, attention_all[3], preferred_element_type=FLOAT).astype(
        BFLOAT
    )
    grad_attended = grad_attended.reshape(local_items, P_SIZE, local_heads, head_dim)
    again_weights = jnp.exp(self_scores(queries, keys_in) - log_norm)
    grad_values = jnp.einsum(
        "ihqt,iqhk->ithk", again_weights.astype(BFLOAT), grad_attended, preferred_element_type=FLOAT
    )
    grad_weights = jnp.einsum(
        "iqhk,ithk->ihqt", grad_attended, values_in, preferred_element_type=FLOAT
    )
    grad_scores = (
        again_weights * (grad_weights - jnp.sum(again_weights * grad_weights, -1, keepdims=True))
    ).astype(BFLOAT)
    grad_queries = (
        jnp.einsum("ihqt,ithk->iqhk", grad_scores, keys_in, preferred_element_type=FLOAT) / root_dim
    )
    grad_keys = (
        jnp.einsum("ihqt,iqhk->ithk", grad_scores, queries, preferred_element_type=FLOAT) / root_dim
    )
    grad_projected = (
        jnp.stack([grad_queries, grad_keys, grad_values], 2)
        .reshape(total_rows, 3 * head_cols)
        .astype(BFLOAT)
    )
    grad_qkv = jnp.einsum("rd,re->de", normed1_all, grad_projected, preferred_element_type=FLOAT)
    grad_qkv = grad_qkv.reshape(D, 3, head_cols).transpose(1, 0, 2)
    grad_normed1 = sum_backward(
        jnp.einsum("re,de->rd", grad_projected, qkv_matrix, preferred_element_type=FLOAT)
    )
    grad_gain1 = jnp.sum(mine(grad_normed1 * unit1), 0)
    grad_residual0 = grad_residual1 + norm_backward(grad_normed1, unit1, inverse1, gains_all[0])
    own_grad = mine(grad_residual0)
    patch_onehot = (rows_share(row_patch)[:, None] == jnp.arange(P_SIZE)[None, :]).astype(FLOAT)
    grad_position = jnp.einsum("rp,rd->pd", patch_onehot, own_grad, precision=HIGHEST)
    grad_lead = jnp.sum(rows_share(lead_rows)[:, None] * own_grad, 0)
    start_grad_all = grad_residual0.astype(BFLOAT)
    grad_mixed = jnp.dot(start_grad_all, out_matrix, preferred_element_type=FLOAT)
    grad_out_mix = jnp.einsum(
        "rd,re->de",
        lax.dynamic_slice_in_dim(start_grad_all, var_start, variable_rows, 0),
        lax.dynamic_slice_in_dim(mixed_rows, var_start, variable_rows, 0),
        preferred_element_type=FLOAT,
    )
    variable_weights = jnp.exp(variable_scores - log_total[None])
    grad_mix_weights = jnp.sum(
        (variable_values * grad_mixed[None]).reshape(
            local_vars, total_rows, mixing_heads, head_dim
        ),
        -1,
    )
    weighted_total = jnp.sum(
        (mixed_float * grad_mixed).reshape(total_rows, mixing_heads, head_dim), -1
    )
    grad_variable_scores = (variable_weights * (grad_mix_weights - weighted_total[None])).astype(
        BFLOAT
    )
    grad_variable_values = (widen(variable_weights) * grad_mixed[None]).astype(BFLOAT)
    grad_value_matrix = jnp.einsum(
        "jrd,jre->de", embeds, grad_variable_values, preferred_element_type=FLOAT
    )
    grad_key_query = (
        jnp.einsum("jrd,jrh->dh", embeds, grad_variable_scores, preferred_element_type=FLOAT)
        / root_dim
    )
    grad_key_matrix = (grad_key_query[:, :, None] * query_local[None]).reshape(D, mixing_cols)
    grad_query = jnp.einsum(
        "dhk,dh->hk",
        key_matrix.astype(FLOAT).reshape(D, mixing_heads, head_dim),
        grad_key_query,
        precision=HIGHEST,
    ).reshape(mixing_cols)
    value_side = jnp.einsum(
        "ijcp,jipe->jce",
        field_ones,
        grad_variable_values.reshape(local_vars, local_items, P_SIZE, mixing_cols),
        preferred_element_type=FLOAT,
    )
    score_side = jnp.einsum(
        "ijcp,jiph->jch",
        field_ones,
        grad_variable_scores.reshape(local_vars, local_items, P_SIZE, mixing_heads),
        preferred_element_type=FLOAT,
    )
    grad_slots = (
        jnp.einsum("jce,de->jcd", value_side, value_matrix.astype(FLOAT), precision=HIGHEST)
        + jnp.einsum("jch,dh->jcd", score_side, key_query.astype(FLOAT), precision=HIGHEST)
        / root_dim
    )
    grad_embed = jnp.einsum("jv,jcd->vcd", slot_pick, grad_slots, precision=HIGHEST).reshape(
        VARS * (PIX + 1), D
    )
    query_row = lax.dynamic_update_slice_in_dim(jnp.zeros((D,), FLOAT), grad_query, mp_start, 0)
    grad_gains = jnp.stack([grad_gain1, grad_gain2, grad_gain3, grad_lead, query_row], 0)
    grad_attention = jnp.concatenate([grad_qkv, grad_out_proj[None]], 0)
    grad_dense = jnp.stack([grad_up, grad_down], 0)
    grad_attention, grad_dense = (
        lax.psum_scatter(
            grad_attention.astype(jnp.bfloat16), "dp", scatter_dimension=1, tiled=True
        ).astype(jnp.float32),
        lax.psum_scatter(
            grad_dense.astype(jnp.bfloat16), "dp", scatter_dimension=1, tiled=True
        ).astype(jnp.float32),
    )
    grad_mixing = lax.psum_scatter(
        jnp.stack([grad_key_matrix, grad_value_matrix, grad_out_mix], 0),
        ("dp", "var"),
        scatter_dimension=1,
        tiled=True,
    )
    grad_gains, grad_position, grad_head, grad_embed = (
        lax.psum_scatter(grad_gains, ("dp", "var", "mp"), scatter_dimension=1, tiled=True),
        lax.psum_scatter(grad_position, ("dp", "var", "mp"), scatter_dimension=1, tiled=True),
        lax.psum_scatter(grad_head, ("dp", "var", "mp"), scatter_dimension=1, tiled=True),
        lax.psum_scatter(grad_embed, ("dp", "var", "mp"), scatter_dimension=1, tiled=True),
    )
    grads = (
        grad_attention,
        grad_dense,
        grad_mixing,
        grad_gains,
        grad_position,
        grad_head,
        grad_embed,
    )
    square_sum = sum((jnp.sum(gradient * gradient) for gradient in grads))
    stream_sums = jnp.stack(
        [
            jnp.sum(mine(start_rows) ** 2),
            jnp.sum(mine(attend_out) ** 2),
            jnp.sum(mine(dense_out) ** 2),
            jnp.sum(mine(residual2) ** 2),
        ]
    )
    total_square, loss_value, stream_total = lax.psum(
        (square_sum, loss_part, stream_sums), ("dp", "var", "mp")
    )
    grad_norm = jnp.sqrt(total_square)
    clip_at = 0.25 * math.sqrt(D / (VARS * PIX * items_all * P_SIZE))
    factor = jnp.minimum(1.0, clip_at / grad_norm)
    step_value = step_count.astype(FLOAT)
    matrix_rate = 0.5 / math.sqrt(D)
    weights = (
        attention_weight,
        dense_weight,
        mixing_weight,
        norm_gains,
        position_table,
        head_weight,
        embed_table,
    )
    moments = (
        attention_moment,
        dense_moment,
        mixing_moment,
        gains_moment,
        position_moment,
        head_moment,
        embed_moment,
    )
    squares = (
        attention_square,
        dense_square,
        mixing_square,
        gains_square,
        position_square,
        head_square,
        embed_square,
    )
    rates = (matrix_rate, matrix_rate, matrix_rate, 0.2, 0.2, matrix_rate, 0.2)
    decays = (DECAY, DECAY, DECAY, 0.0, DECAY, DECAY, DECAY)
    updated = []
    for index in range(7):
        updated.extend(
            adam_update(
                weights[index],
                grads[index],
                moments[index],
                squares[index],
                factor,
                step_value,
                rates[index],
                decays[index],
            )
        )
    stream_rms = jnp.sqrt(stream_total / (items_all * P_SIZE * D))
    return (
        loss_value,
        grad_norm,
        updated[0],
        updated[1],
        updated[2],
        updated[3],
        updated[4],
        updated[5],
        updated[6],
        updated[7],
        updated[8],
        updated[9],
        updated[10],
        updated[11],
        updated[12],
        updated[13],
        updated[14],
        updated[15],
        updated[16],
        updated[17],
        updated[18],
        updated[19],
        updated[20],
        stream_rms,
    )


def solution(mesh):
    return jax.shard_map(
        body,
        mesh=mesh,
        in_specs=(
            P("dp", "var", None, None),
            P("dp", None, None),
            P("dp"),
            P(),
            P("var"),
            P(),
            P(None, "dp", ("var", "mp")),
            P(None, "dp", ("var", "mp")),
            P(None, "dp", ("var", "mp")),
            P(None, "dp", ("var", "mp")),
            P(None, "dp", ("var", "mp")),
            P(None, "dp", ("var", "mp")),
            P(None, ("dp", "var"), "mp"),
            P(None, ("dp", "var"), "mp"),
            P(None, ("dp", "var"), "mp"),
            P(None, ("dp", "var", "mp")),
            P(None, ("dp", "var", "mp")),
            P(None, ("dp", "var", "mp")),
            P(None, ("dp", "var", "mp")),
            P(None, ("dp", "var", "mp")),
            P(None, ("dp", "var", "mp")),
            P(None, ("dp", "var", "mp")),
            P(None, ("dp", "var", "mp")),
            P(None, ("dp", "var", "mp")),
            P(None, ("dp", "var", "mp")),
            P(None, ("dp", "var", "mp")),
            P(None, ("dp", "var", "mp")),
        ),
        out_specs=(
            P(),
            P(),
            P(None, "dp", ("var", "mp")),
            P(None, "dp", ("var", "mp")),
            P(None, "dp", ("var", "mp")),
            P(None, "dp", ("var", "mp")),
            P(None, "dp", ("var", "mp")),
            P(None, "dp", ("var", "mp")),
            P(None, ("dp", "var"), "mp"),
            P(None, ("dp", "var"), "mp"),
            P(None, ("dp", "var"), "mp"),
            P(None, ("dp", "var", "mp")),
            P(None, ("dp", "var", "mp")),
            P(None, ("dp", "var", "mp")),
            P(None, ("dp", "var", "mp")),
            P(None, ("dp", "var", "mp")),
            P(None, ("dp", "var", "mp")),
            P(None, ("dp", "var", "mp")),
            P(None, ("dp", "var", "mp")),
            P(None, ("dp", "var", "mp")),
            P(None, ("dp", "var", "mp")),
            P(None, ("dp", "var", "mp")),
            P(None, ("dp", "var", "mp")),
            P(),
        ),
        check_vma=False,
    )
```

profile of v0, /device:TPU:0, one launch (start us, length us, event | category | flops | bytes accessed | tf_op | source)
XLA Modules:
  0.0 1545.0 jit_solution(12386919846086079826)
XLA Ops:
  10.0 71.2 %all-gather.3 = f32[32,32,5]{1,2,0:T(8,128)S(1)} all-gather(f32[1,32,5]{1,2,0:T(8,128)} %bitcast.355), channel_id=1, replica_groups=mesh['dp'=2,'var'=4,'mp'=4] {'dp','var','mp'}, dimensions={0}, use_global_device_ids=true | all-gather | bytes 21120 | tf_op jit(solution)/shard_map/all_gather | solution.py:169
  83.8 73.6 %all_gather.33 = f32[240,1024]{0,1:T(8,128)S(1)} all-gather(f32[240,32]{0,1:T(8,128)} %param.53), channel_id=1, replica_groups=mesh['dp'=2,'var'=4,'mp'=4] {'dp','var','mp'}, dimensions={1}, use_global_device_ids=true | all-gather | bytes 1013760 | tf_op jit(solution)/shard_map/all_gather | solution.py:172
  158.9 23.3 %convolution_convert_fusion = bf16[12,2,512,1024]{3,2,1,0:T(8,128)(2,1)} fusion(f32[12,5,1024,1]{2,0,1,3:T(8,128)S(1)} %convolution_bitcast_fusion.2, bf16[2,12,4,512]{3,2,1,0:T(4,128)(2,1)S(1)} %copy-done.55), kind=kOutput, calls=%fused_computation.12 | convolution fusion | flops 767557632 | bytes 25509888 | tf_op jit(solution)/shard_map/ijcp,jcd->jipd/dot_general | solution.py:182
  183.6 11.6 fusion.126
  195.3 14.5 fusion.3
  210.7 5.4 all-gather
  216.1 5.5 all-gather.1
  221.5 7.5 all-gather.15.cloned.1.call-done
  234.3 5.6 while.19
  244.3 9.1 all_gather.40
  253.4 34.8 %all-gather.11.cloned.1.call-done = f32[512,1024]{0,1:T(8,128)} async-done(((f32[512,32]{0,1:T(8,128)}), f32[512,1024]{0,1:T(8,128)}) %all-gather.11.cloned.1.call-update) | async-done | bytes 2097168 | tf_op jit(solution)/shard_map/all_gather | solution.py:170
  291.2 84.3 %all-reduce.8.cloned.1.call-done = bf16[1024,1024]{1,0:T(8,128)(2,1)} async-done(((bf16[1024,1024]{1,0:T(8,128)(2,1)}), bf16[1024,1024]{1,0:T(8,128)(2,1)}) %all-reduce.8.cloned.1.call-update) | async-done | bytes 2097168 | tf_op jit(solution)/shard_map/psum | solution.py:217
  397.1 93.2 %all-reduce.10.cloned.1.call-done = bf16[1024,1024]{1,0:T(8,128)(2,1)} async-done(((bf16[1024,1024]{1,0:T(8,128)(2,1)}), bf16[1024,1024]{1,0:T(8,128)(2,1)}) %all-reduce.10.cloned.1.call-update) | async-done | bytes 2097168 | tf_op jit(solution)/shard_map/psum | solution.py:158
  498.5 6.1 multiply_convert_fusion.6
  510.0 77.0 %all_gather.42 = bf16[192,1024]{0,1:T(8,128)(2,1)} all-gather(bf16[192,32]{0,1:T(8,128)(2,1)S(1)} %convert.54), channel_id=1, replica_groups=mesh['dp'=2,'var'=4,'mp'=4] {'dp','var','mp'}, dimensions={1}, use_global_device_ids=true | all-gather | bytes 405504 | tf_op jit(solution)/shard_map/all_gather | solution.py:171
  587.0 19.7 %all-reduce.12.cloned.1.call-done = bf16[1024,1024]{1,0:T(8,128)(2,1)} async-done(((bf16[1024,1024]{1,0:T(8,128)(2,1)}), bf16[1024,1024]{1,0:T(8,128)(2,1)}) %all-reduce.12.cloned.1.call-update) | async-done | bytes 2097168 | tf_op jit(solution)/shard_map/psum | solution.py:158
  629.5 97.2 %all-reduce.14.cloned.1.call-done = bf16[1024,1024]{1,0:T(8,128)(2,1)} async-done(((bf16[1024,1024]{1,0:T(8,128)(2,1)}), bf16[1024,1024]{1,0:T(8,128)(2,1)}) %all-reduce.14.cloned.1.call-update) | async-done | bytes 2097168 | tf_op jit(solution)/shard_map/psum | solution.py:161
  764.2 77.0 %all-reduce.16.cloned.1.call-done = bf16[1024,1024]{1,0:T(8,128)(2,1)} async-done(((bf16[1024,1024]{1,0:T(8,128)(2,1)}), bf16[1024,1024]{1,0:T(8,128)(2,1)}) %all-reduce.16.cloned.1.call-update) | async-done | bytes 2097168 | tf_op jit(solution)/shard_map/psum | solution.py:161
  855.8 5.1 bitcast_reduce_fusion
  861.1 10.0 fusion.27
  880.5 6.2 broadcast_in_dim.43
  886.7 16.9 %reshape.462 = f32[12,2,512,256]{2,1,3,0:T(2,128)} reshape(f32[12,1024,4,64]{1,3,2,0:T(8,128)} %broadcast_in_dim.43) | data formatting | bytes 25165824 | tf_op jit(solution)/shard_map/reshape | solution.py:44
  904.7 7.9 multiply_convert_fusion
  936.0 13.5 convolution_bitcast_fusion.1
  963.2 16.9 %reduce-scatter.20.cloned.1.call-done = f32[192,32]{0,1:T(8,128)} async-done(((f32[192,1024]{0,1:T(8,128)}), f32[192,32]{0,1:T(8,128)}) %reduce-scatter.20.cloned.1.call-update) | async-done | bytes 24592 | tf_op jit(solution)/shard_map/reduce_scatter | solution.py:403
  981.5 12.5 reduce-scatter.12.cloned.1.call-done
  995.7 21.6 %reduce-scatter.14.cloned.1.call-done = bf16[2,512,256]{2,1,0:T(8,128)(2,1)} async-done(((bf16[2,1024,256]{2,1,0:T(8,128)(2,1)}), bf16[2,512,256]{2,1,0:T(8,128)(2,1)}) %reduce-scatter.14.cloned.1.call-update) | async-done | bytes 524304 | tf_op jit(solution)/shard_map/reduce_scatter | solution.py:390
  1020.5 135.2 %reduce-scatter.22.cloned.1.call-done = f32[32,5]{1,0:T(8,128)} async-done(((f32[1024,5]{1,0:T(8,128)}), f32[32,5]{1,0:T(8,128)}) %reduce-scatter.22.cloned.1.call-update) | async-done | bytes 656
  1157.2 134.6 %reduce-scatter.24.cloned.1.call-done = f32[32,240]{1,0:T(8,128)} async-done(((f32[1024,240]{1,0:T(8,128)}), f32[32,240]{1,0:T(8,128)}) %reduce-scatter.24.cloned.1.call-update) | async-done | bytes 30736
  1294.8 135.6 %reduce-scatter.18.cloned.1.call-done = f32[512,32]{0,1:T(8,128)} async-done(((f32[512,1024]{0,1:T(8,128)}), f32[512,32]{0,1:T(8,128)}) %reduce-scatter.18.cloned.1.call-update) | async-done | bytes 65552 | tf_op jit(solution)/shard_map/reduce_scatter | solution.py:402
  1431.9 45.4 %reduce-scatter.16.cloned.1.call-done = f32[3,128,256]{2,1,0:T(8,128)} async-done(((f32[3,1024,256]{2,1,0:T(8,128)}), f32[3,128,256]{2,1,0:T(8,128)}) %reduce-scatter.16.cloned.1.call-update) | async-done | bytes 393232 | tf_op jit(solution)/shard_map/reduce_scatter | solution.py:394
  1482.3 39.8 %all-reduce.1 = (f32[]{:T(128)}, f32[]{:T(128)}, f32[4]{0:T(128)}) all-reduce(f32[]{:T(128)} %fusion.80, f32[]{:T(128)S(6)} %add.331, f32[4]{0:T(128)} %pad_maximum_fusion.3), channel_id=1, replica_groups=mesh['dp'=2,'var'=4,'mp'=4] {'dp','var','mp'}, use_global_device_ids=true, to_apply=%region_20.0 | all-reduce | flops 6 | bytes 48 | tf_op jit(solution)/shard_map/psum | solution.py:424
  (382 shorter events, 207.7 us)
Async XLA Ops:
  8.0 149.9 %copy-start.82 = (s32[12]{0:T(128)S(1)}, s32[12]{0:T(128)}, u32[]{:S(2)}) copy-start(s32[12]{0:T(128)} %param.33) | copy-start | bytes 148
  8.0 150.9 %copy-start.55 = (bf16[2,12,4,512]{3,2,1,0:T(4,128)(2,1)S(1)}, bf16[2,12,4,512]{3,2,1,0:T(4,128)(2,1)}, u32[]{:S(2)}) copy-start(bf16[2,12,4,512]{3,2,1,0:T(4,128)(2,1)} %param.29) | copy-start | bytes 294916
  8.0 174.2 %all-gather.9.cloned.1.call-start = ((), (), s32[]{:S(2)}) async-start(), calls=%async_computation.7 | async-start | bytes 1769472 | tf_op jit(solution)/shard_map/all_gather | solution.py:167
  9.9 219.2 %all-gather.15.cloned.1.call-start = ((), (), s32[]{:S(2)}) async-start(), calls=%async_computation.20 | async-start | bytes 2621440 | tf_op jit(solution)/shard_map/all_gather | solution.py:30
  209.9 78.4 %all-gather.11.cloned.1.call-start = ((), (), s32[]{:S(2)}) async-start(), calls=%async_computation.9 | async-start | bytes 2162688 | tf_op jit(solution)/shard_map/all_gather | solution.py:170
  210.6 164.9 %all-reduce.8.cloned.1.call-start = ((), (), s32[]{:S(2)}) async-start(), calls=%async_computation.8 | async-start | bytes 4194304 | tf_op jit(solution)/shard_map/psum | solution.py:217
  243.5 246.7 %all-reduce.10.cloned.1.call-start = ((), (), s32[]{:S(2)}) async-start(), calls=%async_computation.10 | async-start | bytes 4194304 | tf_op jit(solution)/shard_map/psum | solution.py:158
  253.4 128.5 %copy-start.26 = (bf16[3,1024,64]{1,2,0:T(8,128)(2,1)}, bf16[3,1024,64]{1,2,0:T(8,128)(2,1)S(1)}, u32[]{:S(2)}) copy-start(bf16[3,1024,64]{1,2,0:T(8,128)(2,1)S(1)} %slice.90) | copy-start | bytes 1179652
  389.6 100.6 %copy-start.58 = (f32[1,1024]{1,0:T(1,128)S(1)}, f32[1,1024]{1,0:T(1,128)}, u32[]{:S(2)}) copy-start(f32[1,1024]{1,0:T(1,128)} %get-tuple-element.395) | copy-start | bytes 12292
  389.6 100.6 %copy-start.60 = (f32[1,4,2,128]{3,1,2,0:T(4,128)S(1)}, f32[1,4,2,128]{3,1,2,0:T(4,128)}, u32[]{:S(2)}) copy-start(f32[1,4,2,128]{3,1,2,0:T(4,128)} %copy.270) | copy-start | bytes 12292
  389.8 104.0 %copy-start.43 = (bf16[8,8,2,512]{3,1,2,0:T(8,128)(2,1)}, bf16[8,8,2,512]{3,1,2,0:T(8,128)(2,1)S(1)}, u32[]{:S(2)}) copy-start(bf16[8,8,2,512]{3,1,2,0:T(8,128)(2,1)S(1)} %copy.271) | copy-start | bytes 393220
  392.9 105.6 %all-gather.13.cloned.1.call-start = ((), (), s32[]{:S(2)}) async-start(), calls=%async_computation.11 | async-start | bytes 1572864 | tf_op jit(solution)/shard_map/all_gather | solution.py:165
  395.0 211.7 %all-reduce.12.cloned.1.call-start = ((), (), s32[]{:S(2)}) async-start(), calls=%async_computation.12 | async-start | bytes 4194304 | tf_op jit(solution)/shard_map/psum | solution.py:158
  507.5 219.2 %all-reduce.14.cloned.1.call-start = ((), (), s32[]{:S(2)}) async-start(), calls=%async_computation.13 | async-start | bytes 4194304 | tf_op jit(solution)/shard_map/psum | solution.py:161
  507.9 103.1 %copy-start.76 = (f32[1,4,2,128]{3,1,2,0:T(4,128)}, f32[1,4,2,128]{3,1,2,0:T(4,128)S(1)}, u32[]{:S(2)}) copy-start(f32[1,4,2,128]{3,1,2,0:T(4,128)S(1)} %copy.269) | copy-start | bytes 12292
  629.2 212.0 %all-reduce.16.cloned.1.call-start = ((), (), s32[]{:S(2)}) async-start(), calls=%async_computation.16 | async-start | bytes 4194304 | tf_op jit(solution)/shard_map/psum | solution.py:161
  629.5 106.8 %copy-start.68 = (f32[2,512]{1,0:T(2,128)}, f32[2,512]{1,0:T(2,128)S(1)}, u32[]{:S(2)}) copy-start(f32[2,512]{1,0:T(2,128)S(1)} %log_add_fusion.1) | copy-start | bytes 12292
  743.4 236.7 %reduce-scatter.20.cloned.1.call-start = ((), (), s32[]{:S(2)}) async-start(), calls=%async_computation.19 | async-start | bytes 1081344 | tf_op jit(solution)/shard_map/reduce_scatter | solution.py:403
  746.1 247.9 %reduce-scatter.12.cloned.1.call-start = ((), (), s32[]{:S(2)}) async-start(), calls=%async_computation.14 | async-start | bytes 786432 | tf_op jit(solution)/shard_map/reduce_scatter | solution.py:387
  751.4 265.8 %reduce-scatter.14.cloned.1.call-start = ((), (), s32[]{:S(2)}) async-start(), calls=%async_computation.15 | async-start | bytes 1572864 | tf_op jit(solution)/shard_map/reduce_scatter | solution.py:390
  760.4 395.4 %reduce-scatter.22.cloned.1.call-start = ((), (), s32[]{:S(2)}) async-start(), calls=%async_computation.21 | async-start | bytes 540672
  914.5 377.3 %reduce-scatter.24.cloned.1.call-start = ((), (), s32[]{:S(2)}) async-start(), calls=%async_computation.22 | async-start | bytes 1081344
  921.4 509.0 %reduce-scatter.18.cloned.1.call-start = ((), (), s32[]{:S(2)}) async-start(), calls=%async_computation.18 | async-start | bytes 2162688 | tf_op jit(solution)/shard_map/reduce_scatter | solution.py:402
  925.0 552.4 %reduce-scatter.16.cloned.1.call-start = ((), (), s32[]{:S(2)}) async-start(), calls=%async_computation.17 | async-start | bytes 3538944 | tf_op jit(solution)/shard_map/reduce_scatter | solution.py:394
  955.6 568.5 %copy-start.77 = (f32[5,32]{1,0:T(8,128)S(1)}, f32[5,32]{1,0:T(8,128)}, u32[]{:S(2)}) copy-start(f32[5,32]{1,0:T(8,128)} %param.44) | copy-start | bytes 1924
  955.6 568.5 %copy-start.80 = (f32[5,32]{1,0:T(8,128)S(1)}, f32[5,32]{1,0:T(8,128)}, u32[]{:S(2)}) copy-start(f32[5,32]{1,0:T(8,128)} %param.46) | copy-start | bytes 1924
  955.6 568.5 %copy-start.81 = (f32[5,32]{1,0:T(8,128)S(1)}, f32[5,32]{1,0:T(8,128)}, u32[]{:S(2)}) copy-start(f32[5,32]{1,0:T(8,128)} %param.45) | copy-start | bytes 1924
  955.6 573.6 %copy-start.41 = (f32[3,128,256]{2,1,0:T(8,128)S(1)}, f32[3,128,256]{2,1,0:T(8,128)}, u32[]{:S(2)}) copy-start(f32[3,128,256]{2,1,0:T(8,128)} %param.41) | copy-start | bytes 1179652
  956.1 575.6 %copy-start.38 = (f32[4,512,64]{1,2,0:T(8,128)S(1)}, f32[4,512,64]{1,2,0:T(8,128)}, u32[]{:S(2)}) copy-start(f32[4,512,64]{1,2,0:T(8,128)} %param.35) | copy-start | bytes 1572868
  995.7 538.7 %copy-start.24 = (f32[2,512,256]{2,1,0:T(8,128)S(1)}, f32[2,512,256]{2,1,0:T(8,128)}, u32[]{:S(2)}) copy-start(f32[2,512,256]{2,1,0:T(8,128)} %param.38) | copy-start | bytes 3145732
  995.7 538.7 %copy-start.48 = (f32[2,512,256]{2,1,0:T(8,128)S(1)}, f32[2,512,256]{2,1,0:T(8,128)}, u32[]{:S(2)}) copy-start(f32[2,512,256]{2,1,0:T(8,128)} %param.40) | copy-start | bytes 3145732
  1017.3 517.1 %copy-start.31 = (bf16[2,512,256]{2,1,0:T(8,128)(2,1)S(1)}, bf16[2,512,256]{2,1,0:T(8,128)(2,1)}, u32[]{:S(2)}) copy-start(bf16[2,512,256]{2,1,0:T(8,128)(2,1)} %reduce-scatter.14.cloned.1.call-done) | copy-start | bytes 1572868
  (72 other events, 513.0 us)
Sparse Core Ops, SparseCore 0:
  11.3 28.5 all-gather.8
  210.0 19.0 all-gather.14
  232.1 56.1 all-gather.10
  290.5 84.9 all-reduce.7
  393.0 97.2 all-reduce.9
  507.6 99.0 all-reduce.11
  629.3 97.3 all-reduce.13
  743.5 97.6 all-reduce.15
  843.4 136.6 reduce-scatter.19
  982.8 11.1 reduce-scatter.11
  996.8 20.3 reduce-scatter.13
  1019.9 135.8 reduce-scatter.21
  1158.0 133.7 reduce-scatter.23
  1293.9 136.5 reduce-scatter.17
  1433.7 43.5 reduce-scatter.15
Sparse Core Ops, SparseCore 1:
  395.5 20.1 all-gather.12
where the time goes:
time: 1560 us; the launch traced here: 1540 us
  waiting for transfers between devices  917 us (59%)
  blocking collectives  282 us (18%)
  matrix products  135 us (9%)
  other arithmetic  110 us (7%)
  local copies, waits for them, and re-layouts  75.7 us (5%)
  between operations  24.8 us (2%)
    unnamed x18, waiting for transfers between devices  271 us
    psum x2, waiting for transfers between devices, sum_backward(): lax.psum(partial_rows.astype(jnp.bfloat16), ('var', 'mp'))  174 us
    reduce_scatter x1, waiting for transfers between devices, body(): lax.psum_scatter(grad_position, ('dp', 'var', 'mp'), scatter_dimension=1,...  136 us
    psum x2, waiting for transfers between devices, sum_forward(): lax.psum(partial_rows.astype(jnp.bfloat16), ('var', 'mp'))  113 us
    psum x1, waiting for transfers between devices, body(): lax.psum(start_part.astype(jnp.bfloat16), 'mp').astype(jnp.float32)  84.3 us
    all_gather x1, blocking collectives, body(): lax.all_gather(head_weight, ('dp', 'var', 'mp'), axis=1, tiled=True)  77 us
    all_gather x1, blocking collectives, body(): lax.all_gather(embed_table, ('dp', 'var', 'mp'), axis=1, tiled=True)  73.6 us
    all_gather x1, blocking collectives, body(): lax.all_gather(norm_gains, ('dp', 'var', 'mp'), axis=1, tiled=True)  71.2 us
  transfers between devices with their start and end apart: 16, of which 14 were waited for; matrix products, arithmetic and copies ran while one was open for 14% of the time, Pallas kernels for 0%

commit v1 on v0

v1 whole, which is shorter than its diff:
```python
import math
import types

import jax
import jax.numpy as jnp
from jax import lax
from jax.experimental import pallas as pl
from jax.experimental.pallas import tpu as pltpu
from jax.sharding import PartitionSpec as P

D = 1024
HEADS = 16
VARS = 48
PIX = 4
PH = 16
PW = 32
NSRC = 5
P_SIZE = 512
C_OUT = PIX * VARS
HEAD_DIM = D // HEADS
TERMS = VARS * (PIX + 1)

HIGHEST = lax.Precision.HIGHEST
FLOAT = jnp.float32
BFLOAT = jnp.bfloat16
NORM_EPS = 1e-05
BETA_ONE = 0.5
BETA_TWO = 0.7
ADAM_EPS = 1e-08
DECAY = 0.01
MESH = pl.DeviceIdType.MESH

ROWS = 64
HALF = ROWS // 2
PAIR = 2 * ROWS
PAD = 16
ROOT = math.sqrt(HEAD_DIM)


def place():
    x, w, z = lax.axis_index("dp"), lax.axis_index("var"), lax.axis_index("mp")
    y, c, group, low = lax.div(w, 2), lax.rem(w, 2), lax.div(z, 2), lax.rem(z, 2)
    return types.SimpleNamespace(
        x=x, w=w, z=z, y=y, c=c, group=group, low=low,
        core_peer={"var": 2 * y + (1 - c)},
        y_peer={"var": 2 * (1 - y) + c},
        z_peer={"mp": 2 * group + (1 - low)},
        pair_peer={"mp": 2 * (1 - group) + low},
    )


def sizes():
    dp, var, mp = lax.axis_size("dp"), lax.axis_size("var"), lax.axis_size("mp")
    return types.SimpleNamespace(dp=dp, var=var, mp=mp, plane=dp * var, all=dp * var * mp)


def device_of(index):
    n = sizes()
    return {
        "dp": lax.div(index, n.var * n.mp),
        "var": lax.rem(lax.div(index, n.mp), n.var),
        "mp": lax.rem(index, n.mp),
    }


class Links:
    def __init__(self, send, recv):
        self.send, self.recv, self.used = send, recv, 0
        self.open = []

    def start(self, src, dst, device):
        index = self.used
        self.used += 1
        copy = pltpu.make_async_remote_copy(
            src_ref=src, dst_ref=dst, send_sem=self.send.at[index], recv_sem=self.recv.at[index],
            device_id=device, device_id_type=MESH,
        )
        copy.start()
        self.open.append(copy)
        return copy

    def finish_sends(self):
        for copy in self.open:
            copy.wait_send()
        self.open = []


def wait_all(copies):
    for copy in copies:
        copy.wait_recv()


def at_rows(index, size, unit=None):
    return pl.ds(pl.multiple_of(index * size, unit or size), size)


def wide(value):
    return value.astype(FLOAT)


def dot(a, b, dims=((1,), (0,)), precision=None):
    return lax.dot_general(a, b, (dims, ((), ())), precision=precision, preferred_element_type=FLOAT)


ROWS_ROWS = ((0,), (0,))
COLS_COLS = ((1,), (1,))


def center(values):
    centred = values - jnp.mean(values, -1, keepdims=True)
    inverse = lax.rsqrt(jnp.mean(centred * centred, -1, keepdims=True) + NORM_EPS)
    return centred * inverse, inverse


def norm_backward(grad_out, unit_rows, inverse, gain_row):
    scaled = grad_out * gain_row
    return inverse * (
        scaled
        - jnp.mean(scaled, -1, keepdims=True)
        - unit_rows * jnp.mean(scaled * unit_rows, -1, keepdims=True)
    )


def column_sum(values):
    return jnp.sum(values, 0, keepdims=True)


def gelu(values):
    return 0.5 * values * (1.0 + lax.erf(values * (1.0 / math.sqrt(2.0))))


def gelu_slope(values):
    bell = jnp.exp(-0.5 * values * values) * (1.0 / math.sqrt(2.0 * math.pi))
    return 0.5 * (1.0 + lax.erf(values * (1.0 / math.sqrt(2.0)))) + values * bell


def square_sum(links, p, part, buffers, fill, during=None):
    core_in, held, diag_in, diag_out, last_in = buffers
    sides = (1 - p.y, p.y)
    first = []
    for k, side in enumerate(sides):
        theirs = 2 * side + (1 - p.c)
        fill(theirs)
        first.append(links.start(part.at[at_rows(theirs, PAIR)], core_in.at[k], p.core_peer))
    for side in sides:
        fill(2 * side + p.c)
    for k, side in enumerate(sides):
        first[k].wait_recv()
        held[k] = (wide(part[at_rows(2 * side + p.c, PAIR), :]) + wide(core_in[k])).astype(BFLOAT)

    def piece(which, offset):
        return pl.ds(pl.multiple_of(which * ROWS + offset, HALF), HALF)

    top, end = pl.ds(0, HALF), pl.ds(HALF, HALF)
    diag_z = links.start(held.at[0, piece(1 - p.low, 0)], diag_in.at[0], p.z_peer)
    diag_y = links.start(held.at[0, piece(1 - p.low, HALF)], diag_in.at[1], p.y_peer)
    last = [
        links.start(held.at[0, piece(p.low, HALF)], last_in.at[0, end], p.y_peer),
        links.start(held.at[1, piece(1 - p.low, 0)], last_in.at[1, top], p.z_peer),
    ]
    diag_z.wait_recv()
    diag_out[0] = (wide(held[0, piece(p.low, 0), :]) + wide(diag_in[0])).astype(BFLOAT)
    last.append(links.start(diag_out.at[0], last_in.at[0, top], p.y_peer))
    diag_y.wait_recv()
    diag_out[1] = (wide(held[1, piece(1 - p.low, HALF), :]) + wide(diag_in[1])).astype(BFLOAT)
    last.append(links.start(diag_out.at[1], last_in.at[1, end], p.z_peer))
    if during is not None:
        during()
    wait_all(last)
    return wide(held[1, at_rows(p.low, ROWS), :]) + wide(last_in[0]) + wide(last_in[1])


def square_gather(links, p, out, own_rows, during=None):
    def rows(y, low, offset=0, size=ROWS):
        return out.at[pl.ds(pl.multiple_of((4 * y + 2 * p.c + low) * ROWS + offset, HALF), size)]

    own, from_y, from_z = rows(p.y, p.low), rows(1 - p.y, p.low), rows(p.y, 1 - p.low)
    own[...] = own_rows.astype(BFLOAT)
    y_top, z_end = rows(1 - p.y, p.low, 0, HALF), rows(p.y, 1 - p.low, HALF, HALF)
    far_top, far_end = rows(1 - p.y, 1 - p.low, 0, HALF), rows(1 - p.y, 1 - p.low, HALF, HALF)
    to_y = links.start(own, own, p.y_peer)
    to_z = links.start(own, own, p.z_peer)
    last = [links.start(own, own, p.core_peer)]
    if during is not None:
        during()
    to_y.wait_recv()
    y_to_z = links.start(y_top, y_top, p.z_peer)
    last.append(links.start(from_y, from_y, p.core_peer))
    to_z.wait_recv()
    z_to_y = links.start(z_end, z_end, p.y_peer)
    last.append(links.start(from_z, from_z, p.core_peer))
    y_to_z.wait_recv()
    last.append(links.start(far_top, far_top, p.core_peer))
    z_to_y.wait_recv()
    last.append(links.start(far_end, far_end, p.core_peer))
    wait_all(last)


def plane_sum(links, p, part, total, parts_in, dp_in, held):
    n = sizes()
    rows = part.shape[0] // n.var
    copies = []
    for k in range(1, n.var):
        other = lax.rem(p.w + k, n.var)
        copies.append(links.start(part.at[at_rows(other, rows)], parts_in.at[k - 1], {"var": other}))
    mine = part[at_rows(p.w, rows), :]
    for k, copy in enumerate(copies):
        copy.wait_recv()
        mine = mine + parts_in[k]
    held[...] = mine
    copies = [links.start(held, dp_in.at[k - 1], {"dp": lax.rem(p.x + k, n.dp)}) for k in range(1, n.dp)]
    for k, copy in enumerate(copies):
        copy.wait_recv()
        mine = mine + dp_in[k]
    total[at_rows(p.w, rows), :] = mine
    own = total.at[at_rows(p.w, rows)]
    wait_all([links.start(own, own, {"var": lax.rem(p.w + k, n.var)}) for k in range(1, n.var)])


def stack_rows(target, pieces, count, rows, kind):
    if rows % (16 if kind == BFLOAT else 8) == 0:
        target[...] = pieces[...].reshape(count * rows, pieces.shape[-1]).astype(target.dtype)
    else:
        for k in range(count):
            target[k * rows : (k + 1) * rows, :] = pieces[k].astype(target.dtype)


def step_shapes():
    n = sizes()
    columns = D // n.all
    split = D // n.dp
    plane_rows = D // n.plane
    mix = D // n.mp
    mix_rows = 2 * PAIR
    slots = PAD * n.var
    vmem = pltpu.VMEM
    inputs = [
        "lead_hours", "sources", "latitude", "fields", "target", "attention", "dense", "mixing", "gains", "pos",
        "head", "emb",
    ]
    outs = dict(
        g_attention=((4, HEAD_DIM, split), FLOAT),
        g_dense=((2, split, 256), FLOAT),
        g_mixing=((3, plane_rows, mix), FLOAT),
        g_gains=((5, columns), FLOAT),
        g_pos=((columns, P_SIZE), FLOAT),
        g_head=((columns, C_OUT), FLOAT),
        g_emb=((columns, TERMS), FLOAT),
        totals=((8, 128), FLOAT),
    )
    b, f = BFLOAT, FLOAT
    scratch = dict(
        att=vmem((2, n.dp, 4 * HEAD_DIM, split), b),
        ffw=vmem((2, 2, D, 256), b),
        emb_all=vmem((n.mp, columns, TERMS), f),
        emb_rows=vmem((n.mp * columns, TERMS), f),
        fields_all=vmem((n.var, PIX + 1, PAD, mix_rows), b),
        gains_all=vmem((n.all, 5, columns), f),
        gain_rows=vmem((8, D), f),
        head_own=vmem((columns, C_OUT), b),
        head_all=vmem((n.all, columns, C_OUT), b),
        head_rows=vmem((D, C_OUT), b),
        pos_own=vmem((columns, P_SIZE), b),
        pos_all=vmem((n.all, columns, PAIR), b),
        pos_cols=vmem((D, PAIR), f),
        pos_rows=vmem((PAIR, D), f),
        own_out=vmem((plane_rows, mix), b),
        out_all=vmem((n.plane, plane_rows, mix), b),
        out_rows=vmem((D, mix), b),
        key_query=vmem((plane_rows, 128), f),
        tables_part=vmem((256, mix), f),
        tables=vmem((256, mix), f),
        tables_in=vmem((n.var - 1, 256 // n.var, mix), f),
        tables_dp=vmem((n.dp - 1, 256 // n.var, mix), f),
        tables_held=vmem((256 // n.var, mix), f),
        sides_part=vmem((256, mix), f),
        sides=vmem((256, mix), f),
        sides_in=vmem((n.var - 1, 256 // n.var, mix), f),
        sides_dp=vmem((n.dp - 1, 256 // n.var, mix), f),
        sides_held=vmem((256 // n.var, mix), f),
        pick=vmem(((PIX + 1) * slots, TERMS), f),
        slot_table=vmem(((PIX + 1) * slots, mix), f),
        terms=vmem((PIX, slots, mix_rows), f),
        mix_weights=vmem((mix // HEAD_DIM, slots, mix_rows), f),
        mixed=vmem((mix_rows, mix), b),
        start_part=vmem((mix_rows, D), b),
        start_in=vmem((n.mp - 1, ROWS, D), b),
        start_grad=vmem((mix_rows, D), b),
        part0=vmem((P_SIZE, D), b),
        part1=vmem((P_SIZE, D), b),
        part2=vmem((P_SIZE, D), b),
        part3=vmem((P_SIZE, D), b),
        n1=vmem((P_SIZE, D), b),
        n2=vmem((P_SIZE, D), b),
        g2=vmem((P_SIZE, D), b),
        g1=vmem((P_SIZE, D), b),
        res0=vmem((ROWS, D), f),
        res1=vmem((ROWS, D), f),
        gres=vmem((ROWS, D), f),
        n3=vmem((ROWS, D), b),
        grad_pred=vmem((ROWS, C_OUT), f),
        proj=vmem((2, P_SIZE, 3 * HEAD_DIM), b),
        gproj=vmem((2, P_SIZE, 3 * HEAD_DIM), b),
        weights=vmem((2, P_SIZE, P_SIZE), f),
        dscores=vmem((2, P_SIZE, P_SIZE), b),
        attended=vmem((P_SIZE, 2 * HEAD_DIM), b),
        gattended=vmem((P_SIZE, 2 * HEAD_DIM), b),
        pre=vmem((P_SIZE, 512), f),
        act=vmem((P_SIZE, 512), b),
        gpre=vmem((P_SIZE, 512), b),
        target_own=vmem((ROWS, C_OUT), f),
        ga=vmem((n.dp, 2, 4 * HEAD_DIM, split), b),
        ga_in=vmem((n.dp - 1, 2, 4 * HEAD_DIM, split), b),
        ga_pair=vmem((4 * HEAD_DIM, split), b),
        ga_pair_in=vmem((4 * HEAD_DIM, split), b),
        ga_mine=vmem((4 * HEAD_DIM, split), f),
        gd=vmem((n.dp, 2, 2, split, 256), b),
        gd_in=vmem((n.dp - 1, 2, 2, split, 256), b),
        gd_pair=vmem((2, split, 256), b),
        gd_pair_in=vmem((2, split, 256), b),
        gd_mine=vmem((2, split, 256), f),
        gh=vmem((n.all, columns, C_OUT), b),
        gh_in=vmem((n.all, columns, C_OUT), b),
        gp=vmem((n.all, columns, PAIR), f),
        gp_in=vmem((n.plane, columns, PAIR), f),
        gp_sum=vmem((columns, PAIR), f),
        gp_all=vmem((n.var, columns, PAIR), f),
        ge=vmem((n.mp, columns, TERMS), f),
        ge_in=vmem((n.mp, columns, TERMS), f),
        gw=vmem((n.plane, plane_rows, mix), b),
        gw_in=vmem((n.plane, plane_rows, mix), b),
        gg=vmem((8, D), f),
        gg_in=vmem((n.all, 8, 128), f),
        tile=vmem((8, 128), f),
        tiles=vmem((n.all, 8, 128), f),
    )
    for k in range(4):
        scratch.update(
            {
                f"core_in{k}": vmem((2, PAIR, D), b),
                f"held{k}": vmem((2, PAIR, D), b),
                f"diag_in{k}": vmem((2, HALF, D), b),
                f"diag_out{k}": vmem((2, HALF, D), b),
                f"last_in{k}": vmem((2, ROWS, D), b),
            }
        )
    count = 160 + 12 * n.dp
    scratch.update(
        send=pltpu.SemaphoreType.DMA((count,)),
        recv=pltpu.SemaphoreType.DMA((count,)),
        send_all=pltpu.SemaphoreType.DMA((4, n.all)),
        recv_all=pltpu.SemaphoreType.DMA((4, n.all)),
        send_plane=pltpu.SemaphoreType.DMA((3, n.plane)),
        recv_plane=pltpu.SemaphoreType.DMA((3, n.plane)),
        local=pltpu.SemaphoreType.DMA((1,)),
    )
    return inputs, outs, scratch


def step_kernel(names, *refs):
    r = types.SimpleNamespace(**dict(zip(names, refs)))
    n, p = sizes(), place()
    x, w, z = p.x, p.w, p.z
    me, plane_me = (x * n.var + w) * n.mp + z, x * n.var + w
    columns, split, plane_rows, mix = D // n.all, D // n.dp, D // n.plane, D // n.mp
    mix_heads, slots = mix // HEAD_DIM, PAD * n.var
    local_vars = VARS // n.var
    links = Links(r.send, r.recv)

    def buffers(k):
        return [getattr(r, f"{name}{k}") for name in ("core_in", "held", "diag_in", "diag_out", "last_in")]

    def everyone(kind, count, make):
        send, recv = (r.send_all, r.recv_all) if count == n.all else (r.send_plane, r.recv_plane)

        def copy(k):
            src, dst, device = make(k)
            return pltpu.make_async_remote_copy(
                src_ref=src, dst_ref=dst, send_sem=send.at[kind, k], recv_sem=recv.at[kind, k],
                device_id=device, device_id_type=MESH,
            )

        def run(action):
            def one(k, _):
                action(copy(k))
                return 0

            lax.fori_loop(1, count, one, 0)

        return run

    def begin(copy):
        copy.start()

    def arrive(copy):
        copy.wait_recv()

    def leave(copy):
        copy.wait_send()

    barrier = pltpu.get_barrier_semaphore()

    def signal(k, _):
        pl.semaphore_signal(
            barrier, inc=1, device_id=device_of(lax.rem(me + k, n.all)), device_id_type=MESH
        )
        return 0

    lax.fori_loop(1, n.all, signal, 0)
    own_target = pltpu.make_async_copy(
        r.target.at[p.group, at_rows(2 * w + p.low, ROWS), :], r.target_own, r.local.at[0]
    )
    own_target.start()
    r.att[p.group, x] = r.attention[...].reshape(4 * HEAD_DIM, split).astype(BFLOAT)
    own_split = at_rows(x, split)
    for k in range(2):
        r.ffw[p.group, k, own_split, :] = r.dense[k].astype(BFLOAT)
    r.own_out[...] = r.mixing[2].astype(BFLOAT)
    r.out_all[plane_me] = r.mixing[2].astype(BFLOAT)
    r.head_own[...] = r.head[...].astype(BFLOAT)
    r.head_all[me] = r.head[...].astype(BFLOAT)
    r.pos_own[...] = r.pos[...].astype(BFLOAT)
    r.pos_all[me] = r.pos[:, at_rows(w, PAIR)].astype(BFLOAT)
    r.emb_all[z] = r.emb[...]
    r.fields_all[w] = r.fields[w]
    r.gains_all[me] = r.gains[...]
    pl.semaphore_wait(barrier, n.all - 1)

    emb_copies = [
        links.start(r.emb, r.emb_all.at[z], {"mp": lax.rem(z + k, n.mp)}) for k in range(1, n.mp)
    ]

    def to_device(k):
        other = lax.rem(me + k, n.all)
        return other, device_of(other)

    def to_plane(k):
        other = lax.rem(plane_me + k, n.plane)
        return other, {"dp": lax.div(other, n.var), "var": lax.rem(other, n.var)}

    gains_run = everyone(0, n.all, lambda k: (r.gains, r.gains_all.at[me], to_device(k)[1]))
    gains_run(begin)
    field_copies = []
    for k in range(1, n.var):
        other = lax.rem(w + k, n.var)
        field_copies.append(links.start(r.fields.at[other], r.fields_all.at[w], {"var": other}))
    att_pair = links.start(r.att.at[p.group, x], r.att.at[p.group, x], p.pair_peer)
    out_run = everyone(0, n.plane, lambda k: (r.own_out, r.out_all.at[plane_me], to_plane(k)[1]))
    out_run(begin)

    def pos_make(k):
        device = to_device(k)[1]
        return r.pos_own.at[:, at_rows(device["var"], PAIR)], r.pos_all.at[me], device

    pos_run = everyone(1, n.all, pos_make)
    pos_run(begin)

    key_own, value_own = wide(r.mixing[0].astype(BFLOAT)), wide(r.mixing[1].astype(BFLOAT))
    wait_all(emb_copies)
    stack_rows(r.emb_rows, r.emb_all, n.mp, columns, FLOAT)
    emb_rows = r.emb_rows[...]
    r.tables_part[0:TERMS, :] = dot(emb_rows, value_own, ROWS_ROWS, HIGHEST)
    gains_run(arrive)
    for k in range(n.all):
        r.gain_rows[0:5, k * columns : (k + 1) * columns] = r.gains_all[k]
    query = r.gain_rows[4:5, at_rows(z, mix)]
    head_of = (
        lax.div(lax.broadcasted_iota(jnp.int32, (mix, 128), 0), HEAD_DIM)
        == lax.broadcasted_iota(jnp.int32, (mix, 128), 1)
    ).astype(FLOAT)
    r.key_query[...] = wide(dot(key_own * query, head_of, precision=HIGHEST).astype(BFLOAT))
    r.tables_part[TERMS:256, :] = jnp.zeros((256 - TERMS, mix), FLOAT)
    score_part = dot(r.key_query[...], emb_rows, ROWS_ROWS, HIGHEST)
    r.tables_part[TERMS : TERMS + 8, 0:TERMS] = score_part[0:8, :]
    plane_sum(links, p, r.tables_part, r.tables, r.tables_in, r.tables_dp, r.tables_held)

    def to_dp(copies, src, dst):
        for k in range(1, n.dp):
            copies.append(links.start(src, dst, {"dp": lax.rem(x + k, n.dp)}))

    att_copies, dense_copies = [], []
    to_dp(att_copies, r.att.at[p.group, x], r.att.at[p.group, x])

    wait_all(field_copies)
    every = r.fields_all[...]
    ids = wide(every[:, PIX, :, 0:1]).reshape(slots, 1)
    term_index = lax.broadcasted_iota(jnp.int32, (slots, TERMS), 1).astype(FLOAT)
    for c in range(PIX + 1):
        r.pick[c * slots : (c + 1) * slots, :] = (term_index == ids * (PIX + 1.0) + c).astype(FLOAT)
    r.slot_table[...] = dot(r.pick[...], r.tables[0:TERMS, :], precision=HIGHEST)
    slot_scores = dot(r.pick[...], r.tables[TERMS : TERMS + 8, 0:TERMS], COLS_COLS, HIGHEST)
    for c in range(PIX):
        r.terms[c] = wide(every[:, c]).reshape(slots, 2 * PAIR)
    used = lax.rem(lax.broadcasted_iota(jnp.int32, (slots, 1), 0), PAD) < local_vars
    terms = [r.terms[c] for c in range(PIX)]
    mixed = []

    def stacked(weights):
        return jnp.concatenate([term * weights for term in terms] + [weights], 0)

    for h in range(mix_heads):
        scores = slot_scores[PIX * slots :, h : h + 1]
        for c in range(PIX):
            scores = scores + terms[c] * slot_scores[c * slots : (c + 1) * slots, h : h + 1]
        scores = jnp.where(used, scores * (1.0 / ROOT), -1e30)
        shifted = jnp.exp(scores - jnp.max(scores, 0, keepdims=True))
        weights = shifted / jnp.sum(shifted, 0, keepdims=True)
        r.mix_weights[h] = weights
        mixed.append(
            dot(stacked(weights), r.slot_table[:, h * HEAD_DIM : (h + 1) * HEAD_DIM], ROWS_ROWS, HIGHEST)
        )
    r.mixed[...] = jnp.concatenate(mixed, 1).astype(BFLOAT)
    out_run(arrive)
    stack_rows(r.out_rows, r.out_all, n.plane, plane_rows, BFLOAT)
    r.start_part[...] = dot(r.mixed[...], r.out_rows[...], COLS_COLS).astype(BFLOAT)
    start_copies = []
    for k in range(1, n.mp):
        other = lax.rem(z + k, n.mp)
        start_copies.append(
            links.start(r.start_part.at[at_rows(other, ROWS)], r.start_in.at[k - 1], {"mp": other})
        )
    to_dp(dense_copies, r.ffw.at[p.group, :, own_split], r.ffw.at[p.group, :, own_split])
    att_pair.wait_recv()
    to_dp(att_copies, r.att.at[1 - p.group, x], r.att.at[1 - p.group, x])
    pos_run(arrive)
    stack_rows(r.pos_cols, r.pos_all, n.all, columns, BFLOAT)
    r.pos_rows[...] = r.pos_cols[...].T
    lead = r.lead_hours[p.group].astype(FLOAT) / 100.0
    start = wide(r.start_part[at_rows(z, ROWS), :])
    for k, copy in enumerate(start_copies):
        copy.wait_recv()
        start = start + wide(r.start_in[k])
    start_square = column_sum(start * start)
    residual = start + r.pos_rows[at_rows(p.low, ROWS), :] + lead * r.gain_rows[3:4, :]
    r.res0[...] = residual
    unit, _ = center(residual)
    dense_pair = [links.start(r.ffw.at[p.group, 0, own_split], r.ffw.at[p.group, 0, own_split], p.pair_peer)]
    square_gather(links, p, r.n1, unit * r.gain_rows[0:1, :])
    dense_pair.append(
        links.start(r.ffw.at[p.group, 1, own_split], r.ffw.at[p.group, 1, own_split], p.pair_peer)
    )
    head_run = everyone(2, n.all, lambda k: (r.head_own, r.head_all.at[me], to_device(k)[1]))
    head_run(begin)

    wait_all(att_copies)
    qkv = 3 * HEAD_DIM
    for s in range(2):
        total = dot(r.n1[:, 0:split], r.att[s, 0, 0:qkv, :], COLS_COLS)
        for k in range(1, n.dp):
            total = total + dot(r.n1[:, k * split : (k + 1) * split], r.att[s, k, 0:qkv, :], COLS_COLS)
        r.proj[s] = total.astype(BFLOAT)

    def head_cols(s, which):
        return r.proj[s, :, which * HEAD_DIM : (which + 1) * HEAD_DIM]

    def attention_rows(index):
        rows = at_rows(index, PAIR)
        for s in range(2):
            queries = r.proj[s, rows, 0:HEAD_DIM]
            scores = dot(queries, head_cols(s, 1), COLS_COLS) * (1.0 / ROOT)
            shifted = jnp.exp(scores - jnp.max(scores, -1, keepdims=True))
            weights = shifted / jnp.sum(shifted, -1, keepdims=True)
            r.weights[s, rows, :] = weights
            r.attended[rows, s * HEAD_DIM : (s + 1) * HEAD_DIM] = dot(
                weights.astype(BFLOAT), head_cols(s, 2)
            ).astype(BFLOAT)
        for k in range(n.dp):
            both = jnp.concatenate([r.att[0, k, qkv:, :], r.att[1, k, qkv:, :]], 0)
            r.part0[rows, k * split : (k + 1) * split] = dot(r.attended[rows, :], both).astype(BFLOAT)

    attend = square_sum(links, p, r.part0, buffers(0), attention_rows)
    attend_square = column_sum(attend * attend)
    residual = r.res0[...] + attend
    r.res1[...] = residual
    unit, _ = center(residual)
    wait_all(dense_pair)
    for k in range(2):
        to_dp(dense_copies, r.ffw.at[1 - p.group, k, own_split], r.ffw.at[1 - p.group, k, own_split])
    square_gather(links, p, r.n2, unit * r.gain_rows[1:2, :])

    wait_all(dense_copies)
    hidden = [slice(s * 256, (s + 1) * 256) for s in range(2)]

    def forward_rows(index):
        rows = at_rows(index, PAIR)
        total = None
        for s in range(2):
            pre = dot(r.n2[rows, :], r.ffw[s, 0])
            r.pre[rows, hidden[s]] = pre
            act = gelu(pre).astype(BFLOAT)
            r.act[rows, hidden[s]] = act
            down = dot(act, r.ffw[s, 1], COLS_COLS)
            total = down if total is None else total + down
        r.part1[rows, :] = total.astype(BFLOAT)

    dense = square_sum(links, p, r.part1, buffers(1), forward_rows)
    dense_square = column_sum(dense * dense)
    residual = r.res1[...] + dense
    last_square = column_sum(residual * residual)
    unit, inverse = center(residual)
    head_run(arrive)
    stack_rows(r.head_rows, r.head_all, n.all, columns, BFLOAT)
    normed = (unit * r.gain_rows[2:3, :]).astype(BFLOAT)
    r.n3[...] = normed
    own_source = r.sources[x * 2 + p.group]
    count = jnp.float32(0.0)
    for k in range(r.sources.shape[0]):
        count = count + jnp.where(r.sources[k] == own_source, 1.0, 0.0)
    scale = 1.0 / (NSRC * P_SIZE * C_OUT * count)
    block = 2 * w + p.low
    first_half = lax.broadcasted_iota(jnp.int32, (ROWS, 1), 0) < PW
    row_weight = jnp.where(first_half, r.latitude[2 * block], r.latitude[2 * block + 1]) * scale
    own_target.wait()
    errors = dot(normed, r.head_rows[...]) - r.target_own[...]
    weighted = row_weight * errors
    loss_row = column_sum(weighted * errors)
    grad_pred = 2.0 * weighted
    r.grad_pred[...] = grad_pred
    grad_normed = dot(grad_pred, wide(r.head_rows[...]), COLS_COLS, HIGHEST)
    r.gg[2:3, :] = column_sum(grad_normed * unit)
    grad = norm_backward(grad_normed, unit, inverse, r.gain_rows[2:3, :])
    r.gres[...] = grad

    def head_grads():
        grad_head = dot(wide(r.n3[...]), r.grad_pred[...], ROWS_ROWS, HIGHEST).astype(BFLOAT)
        if columns % 16 == 0:
            r.gh[...] = grad_head.reshape(n.all, columns, C_OUT)
        else:
            for k in range(n.all):
                r.gh[k] = grad_head[k * columns : (k + 1) * columns]

    square_gather(links, p, r.g2, grad, head_grads)
    r.gh_in[me] = r.gh[me]

    def gh_make(k):
        other, device = to_device(k)
        return r.gh.at[other], r.gh_in.at[me], device

    gh_run = everyone(3, n.all, gh_make)
    gh_run(begin)

    def backward_rows(index):
        rows = at_rows(index, PAIR)
        total = None
        for s in range(2):
            grad_act = dot(r.g2[rows, :], r.ffw[s, 1])
            grad_pre = (grad_act * gelu_slope(r.pre[rows, hidden[s]])).astype(BFLOAT)
            r.gpre[rows, hidden[s]] = grad_pre
            back = dot(grad_pre, r.ffw[s, 0], COLS_COLS)
            total = back if total is None else total + back
        r.part2[rows, :] = total.astype(BFLOAT)

    def dense_grads(which):
        for s in range(2):
            if which == 1:
                grad = dot(r.g2[...], r.act[:, hidden[s]], ROWS_ROWS)
            else:
                grad = dot(r.n2[...], r.gpre[:, hidden[s]], ROWS_ROWS)
            for k in range(n.dp):
                r.gd[k, s, which] = grad[k * split : (k + 1) * split].astype(BFLOAT)

    grad_normed = square_sum(links, p, r.part2, buffers(2), backward_rows, lambda: dense_grads(1))
    unit, inverse = center(r.res1[...])
    r.gg[1:2, :] = column_sum(grad_normed * unit)
    grad = r.gres[...] + norm_backward(grad_normed, unit, inverse, r.gain_rows[1:2, :])
    r.gres[...] = grad
    square_gather(links, p, r.g1, grad, lambda: dense_grads(0))

    def over_dp(src, dst):
        return [
            links.start(src.at[lax.rem(x + k, n.dp)], dst.at[k - 1], {"dp": lax.rem(x + k, n.dp)})
            for k in range(1, n.dp)
        ]

    gd_copies = over_dp(r.gd, r.gd_in)

    for s in range(2):
        total = dot(r.g1[:, 0:split], r.att[s, 0, qkv:, :], COLS_COLS)
        for k in range(1, n.dp):
            total = total + dot(r.g1[:, k * split : (k + 1) * split], r.att[s, k, qkv:, :], COLS_COLS)
        r.gattended[:, s * HEAD_DIM : (s + 1) * HEAD_DIM] = total.astype(BFLOAT)

    def score_rows(index, _):
        rows = at_rows(index, PAIR)
        for s in range(2):
            grad_att = r.gattended[rows, s * HEAD_DIM : (s + 1) * HEAD_DIM]
            change = dot(grad_att, head_cols(s, 2), COLS_COLS)
            weights = r.weights[s, rows, :]
            grad_scores = (
                weights * (change - jnp.sum(weights * change, -1, keepdims=True))
            ).astype(BFLOAT)
            r.dscores[s, rows, :] = grad_scores
            r.gproj[s, rows, 0:HEAD_DIM] = (dot(grad_scores, head_cols(s, 1)) * (1.0 / ROOT)).astype(BFLOAT)
        return 0

    lax.fori_loop(0, P_SIZE // PAIR, score_rows, 0)
    for s in range(2):
        r.gproj[s, :, HEAD_DIM : 2 * HEAD_DIM] = (
            dot(r.dscores[s], head_cols(s, 0), ROWS_ROWS) * (1.0 / ROOT)
        ).astype(BFLOAT)
        r.gproj[s, :, 2 * HEAD_DIM :] = dot(
            r.weights[s].astype(BFLOAT), r.gattended[:, s * HEAD_DIM : (s + 1) * HEAD_DIM], ROWS_ROWS
        ).astype(BFLOAT)

    wait_all(gd_copies)

    def summed(own, incoming, s):
        total = wide(own[s])
        for k in range(n.dp - 1):
            total = total + wide(incoming[k, s])
        return total

    gd_own = r.gd.at[x]
    r.gd_mine[...] = summed(gd_own, r.gd_in, p.group)
    r.gd_pair[...] = summed(gd_own, r.gd_in, 1 - p.group).astype(BFLOAT)
    gd_pair = links.start(r.gd_pair, r.gd_pair_in, p.pair_peer)

    def entry_rows(index):
        rows = at_rows(index, PAIR)
        for k in range(n.dp):
            total = dot(r.gproj[0, rows, :], r.att[0, k, 0:qkv, :]) + dot(
                r.gproj[1, rows, :], r.att[1, k, 0:qkv, :]
            )
            r.part3[rows, k * split : (k + 1) * split] = total.astype(BFLOAT)

    def attention_grads():
        for s in range(2):
            grad = dot(r.gproj[s], r.n1[...], ROWS_ROWS)
            for k in range(n.dp):
                r.ga[k, s, 0:qkv, :] = grad[:, k * split : (k + 1) * split].astype(BFLOAT)
        grad = dot(r.attended[...], r.g1[...], ROWS_ROWS)
        for s in range(2):
            for k in range(n.dp):
                r.ga[k, s, qkv:, :] = grad[
                    s * HEAD_DIM : (s + 1) * HEAD_DIM, k * split : (k + 1) * split
                ].astype(BFLOAT)

    grad_normed = square_sum(links, p, r.part3, buffers(3), entry_rows, attention_grads)
    unit, inverse = center(r.res0[...])
    r.gg[0:1, :] = column_sum(grad_normed * unit)
    grad = r.gres[...] + norm_backward(grad_normed, unit, inverse, r.gain_rows[0:1, :])
    r.gg[3:4, :] = lead * column_sum(grad)
    own_rows = r.start_grad.at[at_rows(z, ROWS)]
    own_rows[...] = grad.astype(BFLOAT)
    grad_copies = [
        links.start(own_rows, own_rows, {"mp": lax.rem(z + k, n.mp)}) for k in range(1, n.mp)
    ]
    ga_copies = over_dp(r.ga, r.ga_in)
    wait_all(grad_copies)

    grads = r.start_grad[...]
    grad_mixed = dot(grads, r.out_rows[...])
    for h in range(mix_heads):
        cols = slice(h * HEAD_DIM, (h + 1) * HEAD_DIM)
        weights = r.mix_weights[h]
        through = dot(r.slot_table[:, cols], grad_mixed[:, cols], COLS_COLS, HIGHEST)
        change = through[PIX * slots :]
        for c in range(PIX):
            change = change + terms_of(r, c) * through[c * slots : (c + 1) * slots]
        grad_scores = weights * (change - jnp.sum(weights * change, 0, keepdims=True))
        stack = jnp.concatenate([terms_of(r, c) * weights for c in range(PIX)] + [weights], 0)
        r.side_slots[:, cols] = dot(stack, grad_mixed[:, cols], precision=HIGHEST)
        for c in range(PIX + 1):
            value = terms_of(r, c) * grad_scores if c < PIX else grad_scores
            r.score_slots[c * slots : (c + 1) * slots, h : h + 1] = jnp.sum(value, 1, keepdims=True) * (
                1.0 / ROOT
            )
    r.sides_part[0:TERMS, :] = dot(r.pick[...], r.side_slots[...], ROWS_ROWS, HIGHEST)
    r.sides_part[TERMS:256, :] = jnp.zeros((256 - TERMS, mix), FLOAT)
    r.sides_part[TERMS : TERMS + 8, 0:TERMS] = dot(r.score_slots[...], r.pick[...], ROWS_ROWS, HIGHEST)[0:8, :]
    items = wide(grads[0:PAIR, :]) + wide(grads[PAIR:, :])
    by_column = items.T
    if columns % 8 == 0:
        r.gp[...] = by_column.reshape(n.all, columns, PAIR)
    else:
        for k in range(n.all):
            r.gp[k] = by_column[k * columns : (k + 1) * columns]

    def gp_make(k):
        other, device = to_plane(k)
        return r.gp.at[other * n.mp + z], r.gp_in.at[plane_me], device

    r.gp_in[plane_me] = r.gp[me]
    plane_sum(links, p, r.sides_part, r.sides, r.sides_in, r.sides_dp, r.sides_held)
    gp_run = everyone(1, n.plane, gp_make)
    gp_run(begin)
    grad_out = dot(grads, r.mixed[...], ROWS_ROWS).astype(BFLOAT)
    r.gw[...] = grad_out.reshape(n.plane, plane_rows, mix)
    r.gw_in[plane_me] = r.gw[plane_me]

    def gw_make(k):
        other, device = to_plane(k)
        return r.gw.at[other], r.gw_in.at[plane_me], device

    gw_run = everyone(2, n.plane, gw_make)
    gw_run(begin)

    value_total = r.sides[0:TERMS, :]
    score_total = r.sides[TERMS : TERMS + 8, 0:TERMS]
    emb_rows = r.emb_rows[...]
    query = r.gain_rows[4:5, at_rows(z, mix)]
    grad_emb = dot(wide(r.mixing[1].astype(BFLOAT)), value_total, COLS_COLS, HIGHEST) + dot(
        r.key_query[:, 0:8], score_total, precision=HIGHEST
    )
    if columns % 8 == 0:
        r.ge[...] = grad_emb.reshape(n.mp, columns, TERMS)
    else:
        for k in range(n.mp):
            r.ge[k] = grad_emb[k * columns : (k + 1) * columns]
    r.ge_in[z] = r.ge[z]
    emb_copies = []
    for k in range(1, n.mp):
        other = lax.rem(z + k, n.mp)
        emb_copies.append(links.start(r.ge.at[other], r.ge_in.at[z], {"mp": other}))
    grad_kq = dot(emb_rows, score_total, COLS_COLS, HIGHEST)
    spread = jnp.concatenate(
        [jnp.broadcast_to(grad_kq[:, h : h + 1], (plane_rows, HEAD_DIM)) for h in range(mix_heads)], 1
    )
    r.gg[4:5, :] = jnp.zeros((1, D), FLOAT)
    r.gg[4:5, at_rows(z, mix)] = column_sum(wide(r.mixing[0].astype(BFLOAT)) * spread)
    r.gg[5:8, :] = jnp.zeros((3, D), FLOAT)
    lane_group = lax.div(me * columns, 128)

    def gg_make(k):
        other, device = to_device(k)
        return r.gg.at[:, at_rows(lax.div(other * columns, 128), 128)], r.gg_in.at[me], device

    gains_run(leave)
    gg_run = everyone(0, n.all, gg_make)
    gg_run(begin)
    r.gg_in[me] = r.gg[:, at_rows(lane_group, 128)]
    r.g_mixing[0] = spread * query
    r.g_mixing[1] = dot(emb_rows, value_total, precision=HIGHEST)

    wait_all(ga_copies)
    ga_own = r.ga.at[x]
    r.ga_mine[...] = summed(ga_own, r.ga_in, p.group)
    r.ga_pair[...] = summed(ga_own, r.ga_in, 1 - p.group).astype(BFLOAT)
    ga_pair = links.start(r.ga_pair, r.ga_pair_in, p.pair_peer)

    gp_run(arrive)
    r.gp_sum[...] = jnp.zeros((columns, PAIR), FLOAT)
    for v in range(n.var):
        total = r.gp_in[v]
        for k in range(1, n.dp):
            total = total + r.gp_in[k * n.var + v]
        r.g_pos[:, v * PAIR : (v + 1) * PAIR] = total
    gd_pair.wait_recv()
    r.g_dense[...] = r.gd_mine[...] + wide(r.gd_pair_in[...])
    gh_run(arrive)
    r.g_head[...] = lax.fori_loop(
        0, n.all, lambda k, so_far: so_far + wide(r.gh_in[k]), jnp.zeros((columns, C_OUT), FLOAT)
    )
    gw_run(arrive)
    r.g_mixing[2] = lax.fori_loop(
        0, n.plane, lambda k, so_far: so_far + wide(r.gw_in[k]), jnp.zeros((plane_rows, mix), FLOAT)
    )
    wait_all(emb_copies)
    grad_emb = r.ge_in[0]
    for k in range(1, n.mp):
        grad_emb = grad_emb + r.ge_in[k]
    r.g_emb[...] = grad_emb
    gg_run(arrive)
    gains_sum = lax.fori_loop(
        0, n.all, lambda k, so_far: so_far + r.gg_in[k], jnp.zeros((8, 128), FLOAT)
    )
    lane = lax.broadcasted_iota(jnp.int32, (128, columns), 0)
    offset = me * columns - lane_group * 128
    choose = (lane == lax.broadcasted_iota(jnp.int32, (128, columns), 1) + offset).astype(FLOAT)
    r.g_gains[...] = dot(gains_sum, choose, precision=HIGHEST)[0:5, :]
    ga_pair.wait_recv()
    r.g_attention[...] = (r.ga_mine[...] + wide(r.ga_pair_in[...])).reshape(4, HEAD_DIM, split)

    def square(ref):
        return jnp.sum(ref[...] * ref[...])

    squares = sum(
        square(ref)
        for ref in (r.g_attention, r.g_dense, r.g_mixing, r.g_gains, r.g_pos, r.g_head, r.g_emb)
    )
    line = lax.broadcasted_iota(jnp.int32, (8, 128), 0)
    tile = jnp.zeros((8, 128), FLOAT)
    for k, value in enumerate(
        (
            squares, jnp.sum(loss_row), jnp.sum(start_square), jnp.sum(attend_square), jnp.sum(dense_square),
            jnp.sum(last_square),
        )
    ):
        tile = jnp.where(line == k, value, tile)
    r.tile[...] = tile
    r.tiles[me] = tile
    pos_run(leave)
    tile_run = everyone(1, n.all, lambda k: (r.tile, r.tiles.at[me], to_device(k)[1]))
    tile_run(begin)
    for run in (out_run, head_run, gh_run, gp_run, gw_run, gg_run):
        run(leave)
    links.finish_sends()
    tile_run(arrive)
    r.totals[...] = lax.fori_loop(
        0, n.all, lambda k, so_far: so_far + r.tiles[k], jnp.zeros((8, 128), FLOAT)
    )
    tile_run(leave)


def terms_of(r, c):
    return r.terms[c]


def run_step(values):
    inputs, outs, scratch = step_shapes()
    n = sizes()
    mix = D // n.mp
    scratch["side_slots"] = pltpu.VMEM(((PIX + 1) * PAD * n.var, mix), FLOAT)
    scratch["score_slots"] = pltpu.VMEM(((PIX + 1) * PAD * n.var, 128), FLOAT)
    names = inputs + list(outs) + list(scratch)
    spaces = {"lead_hours": pltpu.SMEM, "sources": pltpu.SMEM, "latitude": pltpu.SMEM, "target": pl.ANY}

    def kernel(*refs):
        step_kernel(names, *refs)

    results = pl.pallas_call(
        kernel,
        out_shape=[jax.ShapeDtypeStruct(shape, kind) for shape, kind in outs.values()],
        in_specs=[pl.BlockSpec(memory_space=spaces.get(name, pltpu.VMEM)) for name in inputs],
        out_specs=[pl.BlockSpec(memory_space=pltpu.VMEM)] * len(outs),
        scratch_shapes=list(scratch.values()),
        compiler_params=pltpu.CompilerParams(
            collective_id=0, has_side_effects=True, vmem_limit_bytes=58000 * 1024
        ),
        name="step",
    )(*[values[name] for name in inputs])
    return dict(zip(outs, results))


RATES = (0.5 / math.sqrt(D), 0.5 / math.sqrt(D), 0.5 / math.sqrt(D), 0.2, 0.2, 0.5 / math.sqrt(D), 0.2)
DECAYS = (DECAY, DECAY, DECAY, 0.0, DECAY, DECAY, DECAY)


def update_kernel(items_all, step_count, totals, *refs):
    clip_at = 0.25 * math.sqrt(D / (VARS * PIX * items_all * P_SIZE))
    norm = jnp.sqrt(totals[0:1, 0:1])
    factor = jnp.minimum(1.0, clip_at / norm)
    step_value = jnp.zeros((1, 1), FLOAT) + step_count[0].astype(FLOAT)
    first_scale = 1.0 / (1.0 - jnp.exp(step_value * math.log(BETA_ONE)))
    second_scale = 1.0 / (1.0 - jnp.exp(step_value * math.log(BETA_TWO)))
    loss_out, norm_out, rms_out = refs[28 + 21 :]
    loss_out[...] = totals[1:2, 0:1]
    norm_out[...] = norm
    rms_out[...] = jnp.sqrt(totals[...] * (1.0 / (items_all * P_SIZE * D)))
    for index in range(7):
        weight, first, second, grad = refs[4 * index : 4 * index + 4]
        weight_out, first_out, second_out = refs[28 + 3 * index : 31 + 3 * index]

        def one(w, m, v, g, index=index):
            clipped = g * factor
            m = BETA_ONE * m + (1.0 - BETA_ONE) * clipped
            v = BETA_TWO * v + (1.0 - BETA_TWO) * clipped * clipped
            normalized = m * first_scale / (jnp.sqrt(v * second_scale) + ADAM_EPS)
            return w - RATES[index] * (normalized + DECAYS[index] * w), m, v

        results = one(weight[...], first[...], second[...], grad[...])
        for out, value in zip((weight_out, first_out, second_out), results):
            out[...] = value


def run_update(items_all, step_count, totals, groups):
    arrays = [array for group in groups for array in group]
    outs = [jax.ShapeDtypeStruct(group[0].shape, FLOAT) for group in groups for _ in range(3)]
    outs += [jax.ShapeDtypeStruct((1, 1), FLOAT)] * 2 + [jax.ShapeDtypeStruct((8, 128), FLOAT)]

    def kernel(*refs):
        update_kernel(items_all, *refs)

    return pl.pallas_call(
        kernel,
        out_shape=outs,
        in_specs=[pl.BlockSpec(memory_space=pltpu.SMEM)]
        + [pl.BlockSpec(memory_space=pltpu.VMEM)] * (1 + len(arrays)),
        out_specs=[pl.BlockSpec(memory_space=pltpu.VMEM)] * len(outs),
        compiler_params=pltpu.CompilerParams(vmem_limit_bytes=40000 * 1024),
        name="update",
    )(step_count.reshape(1), totals, *arrays)


def body(
    fields, target, lead_hours, sources, variables, step_count,
    attention_weight, attention_moment, attention_square,
    dense_weight, dense_moment, dense_square,
    mixing_weight, mixing_moment, mixing_square,
    norm_gains, gains_moment, gains_square,
    position_table, position_moment, position_square,
    head_weight, head_moment, head_square,
    embed_table, embed_moment, embed_square,
):
    n = sizes()
    local_items, local_vars = fields.shape[0], fields.shape[1]
    items_all = sources.shape[0]
    angles = (jnp.arange(PH, dtype=FLOAT) + 0.5) * (math.pi / PH) - math.pi / 2
    cosine = jnp.cos(angles)
    mix_rows = 2 * PAIR
    ids = jnp.broadcast_to(variables.astype(BFLOAT)[None, :, None], (1, local_vars, mix_rows))
    send = []
    for v in range(n.var):
        piece = fields[:, :, :, v * PAIR : (v + 1) * PAIR].transpose(2, 1, 0, 3)
        send.append(jnp.concatenate([piece.reshape(PIX, local_vars, mix_rows), ids], 0))
    send = jnp.pad(
        jnp.stack(send), ((0, 0), (0, 0), (0, PAD - local_vars), (0, 0))
    )
    blank = jnp.arange(PAD) >= local_vars
    plane = jnp.arange(PIX + 1) == PIX
    send = jnp.where(
        (blank[None, :] & plane[:, None])[None, :, :, None], jnp.asarray(-100.0, BFLOAT), send
    )

    def turned(array):
        return jnp.swapaxes(array, -1, -2)

    grads = run_step(
        dict(
            lead_hours=lead_hours, sources=sources, latitude=cosine / jnp.mean(cosine), fields=send,
            target=target, attention=turned(attention_weight), dense=dense_weight, mixing=mixing_weight,
            gains=norm_gains, pos=turned(position_table), head=turned(head_weight), emb=turned(embed_table),
        )
    )
    same = lambda array: array
    plan = (
        (turned, attention_weight, attention_moment, attention_square, grads["g_attention"]),
        (same, dense_weight, dense_moment, dense_square, grads["g_dense"]),
        (same, mixing_weight, mixing_moment, mixing_square, grads["g_mixing"]),
        (same, norm_gains, gains_moment, gains_square, grads["g_gains"]),
        (turned, position_table, position_moment, position_square, grads["g_pos"]),
        (turned, head_weight, head_moment, head_square, grads["g_head"]),
        (turned, embed_table, embed_moment, embed_square, grads["g_emb"]),
    )
    groups = [(way(a), way(b), way(c), g) for way, a, b, c, g in plan]
    results = run_update(items_all, step_count, grads["totals"], groups)
    updated = [plan[k // 3][0](results[k]) for k in range(21)]
    loss, norm, rms = results[21:]
    return (loss.reshape(()), norm.reshape(()), *updated, rms[2:6, 0])


def solution(mesh):
    return jax.shard_map(
        body,
        mesh=mesh,
        in_specs=(
            P("dp", "var", None, None),
            P("dp", None, None),
            P("dp"),
            P(),
            P("var"),
            P(),
            P(None, "dp", ("var", "mp")),
            P(None, "dp", ("var", "mp")),
            P(None, "dp", ("var", "mp")),
            P(None, "dp", ("var", "mp")),
            P(None, "dp", ("var", "mp")),
            P(None, "dp", ("var", "mp")),
            P(None, ("dp", "var"), "mp"),
            P(None, ("dp", "var"), "mp"),
            P(None, ("dp", "var"), "mp"),
            P(None, ("dp", "var", "mp")),
            P(None, ("dp", "var", "mp")),
            P(None, ("dp", "var", "mp")),
            P(None, ("dp", "var", "mp")),
            P(None, ("dp", "var", "mp")),
            P(None, ("dp", "var", "mp")),
            P(None, ("dp", "var", "mp")),
            P(None, ("dp", "var", "mp")),
            P(None, ("dp", "var", "mp")),
            P(None, ("dp", "var", "mp")),
            P(None, ("dp", "var", "mp")),
            P(None, ("dp", "var", "mp")),
        ),
        out_specs=(
            P(),
            P(),
            P(None, "dp", ("var", "mp")),
            P(None, "dp", ("var", "mp")),
            P(None, "dp", ("var", "mp")),
            P(None, "dp", ("var", "mp")),
            P(None, "dp", ("var", "mp")),
            P(None, "dp", ("var", "mp")),
            P(None, ("dp", "var"), "mp"),
            P(None, ("dp", "var"), "mp"),
            P(None, ("dp", "var"), "mp"),
            P(None, ("dp", "var", "mp")),
            P(None, ("dp", "var", "mp")),
            P(None, ("dp", "var", "mp")),
            P(None, ("dp", "var", "mp")),
            P(None, ("dp", "var", "mp")),
            P(None, ("dp", "var", "mp")),
            P(None, ("dp", "var", "mp")),
            P(None, ("dp", "var", "mp")),
            P(None, ("dp", "var", "mp")),
            P(None, ("dp", "var", "mp")),
            P(None, ("dp", "var", "mp")),
            P(None, ("dp", "var", "mp")),
            P(),
        ),
        check_vma=False,
    )
```

time: 1560 us -> 286 us (0.18)
  waiting for transfers between devices: 917 us -> 0 us
  blocking collectives: 282 us -> 0 us
  Pallas kernels: 0 us -> 268 us
  matrix products: 135 us -> 0 us
  other arithmetic: 110 us -> 2.09 us
  local copies, waits for them, and re-layouts: 75.7 us -> 12.5 us
  between operations: 24.8 us -> 2.3 us
    psum x5 -> x0, waiting for transfers between devices: 371 us -> none  [the longest x2 174 us: sum_backward(): lax.psum(partial_rows.astype(jnp.bfloat16), ('var', 'mp'))]
    unnamed x18 -> x0, waiting for transfers between devices: 271 us -> none
    pallas_call x0 -> x2, Pallas kernels: none -> 268 us  [the longest x1 264 us: run_step(): pl.pallas_call(kernel, out_shape=[jax.ShapeDtypeStruct(shape, kind) for s...]
    all_gather x6 -> x0, blocking collectives: 242 us -> none  [the longest x1 77 us: body(): lax.all_gather(head_weight, ('dp', 'var', 'mp'), axis=1, tiled=True)]
    reduce_scatter x5 -> x0, waiting for transfers between devices: 232 us -> none  [the longest x1 136 us: body(): lax.psum_scatter(grad_position, ('dp', 'var', 'mp'), scatter_dimension=1,...]
    dot_general x38 -> x0, matrix products: 135 us -> none  [the longest x1 23.3 us: body(): jnp.einsum('ijcp,jcd->jipd', field_ones.astype(FLOAT), slot_table, precis...]
    reduce_sum x30 -> x1, other arithmetic: 50 us -> 0.65 us  [body(): jnp.mean(cosine)]
    all_gather x4 -> x0, waiting for transfers between devices: 42.4 us -> none  [the longest x1 34.8 us: body(): lax.all_gather(position_table, ('dp', 'var', 'mp'), axis=1, tiled=True)]
  transfers between devices with their start and end apart: 16 -> 0, of which waited for: 14 -> 0; matrix products, arithmetic and copies ran while one was open for 14% -> 0% of each run, Pallas kernels for 0% -> 0%
where the time goes in v1:
time: 286 us; the launch traced here: 285 us
  Pallas kernels  268 us (94%)
  local copies, waits for them, and re-layouts  12.5 us (4%)
    pallas_call x1, Pallas kernels, run_step(): pl.pallas_call(kernel, out_shape=[jax.ShapeDtypeStruct(shape, kind) for s...  264 us
    unnamed x61, local copies, waits for them, and re-layouts  10.8 us

profile of v1, /device:TPU:0, one launch (start us, length us, event | category | flops | bytes accessed | tf_op | source)
XLA Modules:
  0.0 284.9 jit_solution(6915933818884048908)
XLA Ops:
  0.7 0.7 fusion.12
  2.6 0.6 broadcast_divide_fusion.refs_2_
  3.2 0.7 copy-done.29
  3.8 0.1 broadcast_and_fusion
  3.9 0.1 broadcast_in_dim.23
  4.0 0.9 slice_bitcast_fusion.3
  4.9 0.0 copy-start.16
  4.9 0.0 copy-start.18
  4.9 0.0 copy-start.19
  5.0 0.0 copy-start.14
  5.0 0.0 copy-start.15
  5.1 0.0 copy-start.12
  5.1 0.0 copy-start.13
  5.1 0.0 copy-start.10
  5.2 0.0 copy-start.9
  5.2 0.8 fusion.7.refs_3_
  6.0 2.6 copy.64.refs_4_
  8.6 264.3 %step.1 = (f32[4,64,512]{2,1,0:T(8,128)}, f32[2,512,256]{2,1,0:T(8,128)}, f32[3,128,256]{2,1,0:T(8,128)}, f32[5,32]{1,0:T(8,128)}, f32[32,512]{1,0:T(8,128)}, /*...) custom-call(s32[2]{0:T(128)} %refs_0_.1, s32[4]{0:T(128)} %refs_1_.1, f32[16]{0:T(128)} %broadcast_divide_fusion.refs_2_, ...), custom_call_target="tpu_custom_call" | custom-call | tf_op jit(solution)/shard_map/step/pallas_call | solution.py:921
  272.9 0.0 copy-start.24
  272.9 0.0 copy-done.20
  272.9 0.0 copy-done.21
  273.1 0.5 copy-done.24
  273.6 1.2 copy-done.5
  274.8 1.0 copy-done.8
  275.9 1.0 copy-done.11
  276.8 0.8 copy-done.17
  277.7 0.8 copy-done.22
  278.4 0.8 copy-done.23
  279.2 0.7 copy-done.27
  279.9 0.7 copy-done.28
  280.5 3.7 %update.1 = (f32[4,64,512]{2,1,0:T(8,128)}, f32[4,64,512]{2,1,0:T(8,128)}, f32[4,64,512]{2,1,0:T(8,128)}, f32[2,512,256]{2,1,0:T(8,128)}, f32[2,512,256]{2,1,0:T...) custom-call(s32[1]{0:T(128)} %bitcast.43.refs_0_, ...), custom_call_target="tpu_custom_call" | custom-call | tf_op jit(solution)/shard_map/update/pallas_call | solution.py:974
  284.2 0.6 slice_reduce_fusion
  (50 shorter events, 0.3 us)
Async XLA Ops:
  3.2 0.7 copy-start.29
  4.0 268.9 %copy-start.20 = (f32[240,32]{0,1:T(8,128)S(1)}, f32[240,32]{0,1:T(8,128)}, u32[]{:S(2)}) copy-start(f32[240,32]{0,1:T(8,128)} %param.52) | copy-start | bytes 92164
  4.0 268.9 %copy-start.21 = (f32[240,32]{0,1:T(8,128)S(1)}, f32[240,32]{0,1:T(8,128)}, u32[]{:S(2)}) copy-start(f32[240,32]{0,1:T(8,128)} %param.53) | copy-start | bytes 92164
  4.0 268.9 %copy-start.25 = (f32[5,32]{1,0:T(8,128)S(1)}, f32[5,32]{1,0:T(8,128)}, u32[]{:S(2)}) copy-start(f32[5,32]{1,0:T(8,128)} %refs_15_.1) | copy-start | bytes 1924
  4.0 268.9 %copy-start.26 = (f32[5,32]{1,0:T(8,128)S(1)}, f32[5,32]{1,0:T(8,128)}, u32[]{:S(2)}) copy-start(f32[5,32]{1,0:T(8,128)} %refs_16_.1) | copy-start | bytes 1924
  4.9 268.1 %copy-start.16 = (f32[512,32]{0,1:T(8,128)S(1)}, f32[512,32]{0,1:T(8,128)}, u32[]{:S(2)}) copy-start(f32[512,32]{0,1:T(8,128)} %param.47) | copy-start | bytes 196612
  4.9 268.1 %copy-start.18 = (f32[192,32]{0,1:T(8,128)S(1)}, f32[192,32]{0,1:T(8,128)}, u32[]{:S(2)}) copy-start(f32[192,32]{0,1:T(8,128)} %param.49) | copy-start | bytes 73732
  4.9 268.1 %copy-start.19 = (f32[192,32]{0,1:T(8,128)S(1)}, f32[192,32]{0,1:T(8,128)}, u32[]{:S(2)}) copy-start(f32[192,32]{0,1:T(8,128)} %param.50) | copy-start | bytes 73732
  5.0 268.0 %copy-start.14 = (f32[240,32]{0,1:T(8,128)S(1)}, f32[240,32]{0,1:T(8,128)}, u32[]{:S(2)}) copy-start(f32[240,32]{0,1:T(8,128)} %param.51) | copy-start | bytes 92164
  5.0 268.0 %copy-start.15 = (f32[512,32]{0,1:T(8,128)S(1)}, f32[512,32]{0,1:T(8,128)}, u32[]{:S(2)}) copy-start(f32[512,32]{0,1:T(8,128)} %param.46) | copy-start | bytes 196612
  5.1 267.9 %copy-start.12 = (f32[512,32]{0,1:T(8,128)S(1)}, f32[512,32]{0,1:T(8,128)}, u32[]{:S(2)}) copy-start(f32[512,32]{0,1:T(8,128)} %param.45) | copy-start | bytes 196612
  5.1 267.9 %copy-start.13 = (f32[192,32]{0,1:T(8,128)S(1)}, f32[192,32]{0,1:T(8,128)}, u32[]{:S(2)}) copy-start(f32[192,32]{0,1:T(8,128)} %param.48) | copy-start | bytes 73732
  5.1 267.9 %copy-start.10 = (f32[3,128,256]{2,1,0:T(8,128)S(1)}, f32[3,128,256]{2,1,0:T(8,128)}, u32[]{:S(2)}) copy-start(f32[3,128,256]{2,1,0:T(8,128)} %refs_12_.1) | copy-start | bytes 1179652
  5.2 267.8 %copy-start.9 = (f32[3,128,256]{2,1,0:T(8,128)S(1)}, f32[3,128,256]{2,1,0:T(8,128)}, u32[]{:S(2)}) copy-start(f32[3,128,256]{2,1,0:T(8,128)} %refs_11_.1) | copy-start | bytes 1179652
  6.0 267.0 %copy-start.4 = (f32[2,512,256]{2,1,0:T(8,128)S(1)}, f32[2,512,256]{2,1,0:T(8,128)}, u32[]{:S(2)}) copy-start(f32[2,512,256]{2,1,0:T(8,128)} %refs_8_.3) | copy-start | bytes 3145732
  6.0 267.0 %copy-start.6 = (f32[4,512,64]{1,2,0:T(8,128)S(1)}, f32[4,512,64]{1,2,0:T(8,128)}, u32[]{:S(2)}) copy-start(f32[4,512,64]{1,2,0:T(8,128)} %param.34) | copy-start | bytes 1572868
  6.0 267.0 %copy-start.7 = (f32[4,512,64]{1,2,0:T(8,128)S(1)}, f32[4,512,64]{1,2,0:T(8,128)}, u32[]{:S(2)}) copy-start(f32[4,512,64]{1,2,0:T(8,128)} %param.35) | copy-start | bytes 1572868
  8.6 264.5 %copy-start = (f32[2,512,256]{2,1,0:T(8,128)S(1)}, f32[2,512,256]{2,1,0:T(8,128)}, u32[]{:S(2)}) copy-start(f32[2,512,256]{2,1,0:T(8,128)} %refs_6_.3) | copy-start | bytes 3145732
  8.6 264.5 %copy-start.1 = (f32[4,512,64]{1,2,0:T(8,128)S(1)}, f32[4,512,64]{1,2,0:T(8,128)}, u32[]{:S(2)}) copy-start(f32[4,512,64]{1,2,0:T(8,128)} %param.33) | copy-start | bytes 1572868
  8.6 264.5 %copy-start.2 = (f32[3,128,256]{2,1,0:T(8,128)S(1)}, f32[3,128,256]{2,1,0:T(8,128)}, u32[]{:S(2)}) copy-start(f32[3,128,256]{2,1,0:T(8,128)} %refs_10_.1) | copy-start | bytes 1179652
  8.6 264.5 %copy-start.3 = (f32[2,512,256]{2,1,0:T(8,128)S(1)}, f32[2,512,256]{2,1,0:T(8,128)}, u32[]{:S(2)}) copy-start(f32[2,512,256]{2,1,0:T(8,128)} %refs_7_.3) | copy-start | bytes 3145732
  272.9 0.7 copy-start.24
  273.6 1.2 copy-start.5
  274.8 1.0 copy-start.8
  275.8 1.0 copy-start.11
  276.8 0.8 copy-start.17
  277.7 0.8 copy-start.22
  278.4 0.8 copy-start.23
  279.2 0.7 copy-start.27
  279.9 0.7 copy-start.28
